TPU v7x, 256 devices: a whole 4x4x8 slice. The times are simulated.
256 devices in a mesh: seq: 32 (over z, y), head: 8 (over x, core).
Axes of the slice: x: 4, y: 4, z: 8, core: 2. Of those that a mesh axis runs over, the one named last changes fastest.
Arguments:
- queries: bfloat16 [16384, 4096], P('seq', 'head'), may hold values from -6 to 6
- keys: bfloat16 [16384, 4096], P('seq', 'head'), may hold values from -6 to 6
- values: bfloat16 [16384, 4096], P('seq', 'head'), may hold values from -6 to 6
- rates: float32 [8, 16384], P('head', 'seq'), may hold values from 0.005 to 0.05
- gain: float32 [4096], P('head'), may hold values from 0.1 to 1.9
- cotangent: bfloat16 [16384, 4096], P('seq', 'head'), may hold values from -6 to 6
- fast_init: float32 [8, 3, 512, 512], P('head'), may hold values from -60 to 60
- first_moment: float32 [8, 3, 512, 512], P('head', None, 'seq'), may hold values from -6 to 6
- second_moment: float32 [8, 3, 512, 512], P('head', None, 'seq'), may hold values from 0.5 to 4
Outputs:
- layer_out: bfloat16 [16384, 4096], P('seq', 'head')
- new_weights: float32 [8, 3, 512, 512], P('head', None, 'seq')
- new_first: float32 [8, 3, 512, 512], P('head', None, 'seq')
- new_second: float32 [8, 3, 512, 512], P('head', None, 'seq')
All inputs are finite; a program needn't handle non-finite values.
Results may differ from a plain program's by a relative error of at most 0.015.
Values may be sent and summed in bfloat16 or wider, within the bound.
No kernel may reach another device: no remote copies, remote signals or barrier semaphores. Data moves between devices by JAX's collectives and lax.ppermute only.
A program may use at most 64 MiB of HBM per device.

v0:
```python
import jax
import jax.numpy as jnp
from jax import lax
from jax.sharding import Mesh
from jax.sharding import PartitionSpec as P

WIN = 256
WIDTH = 4096
Z = ("zh", "zl")
SEQ = ("zh", "zl", "y")
HEAD = ("x", "c")
NY = 4
NZ = 8
beta_one = 0.9
beta_two = 0.95
adam_rate = 0.02
bf16 = jnp.bfloat16
f32 = jnp.float32


def mm(a, b, ca, cb):
    return lax.dot_general(
        a.astype(bf16), b.astype(bf16), (((ca,), (cb,)), ((), ())), preferred_element_type=f32
    )


def swapped(parts, axes):
    return lax.all_to_all(parts, axes, split_axis=0, concat_axis=0, tiled=True)


def reduce_rows(grads):
    count, _, width = grads.shape
    blocks = grads.astype(bf16).reshape(count, NZ, NY, -1, width)
    got = swapped(jnp.transpose(blocks, (2, 0, 1, 3, 4)), "y")
    total = jnp.sum(got.astype(f32), axis=0)
    got = swapped(jnp.transpose(total.astype(bf16), (1, 0, 2, 3)), Z)
    return jnp.sum(got.astype(f32), axis=0)


def gather_rows(rows):
    count, _, width = rows.shape
    block = swapped(jnp.broadcast_to(rows, (4, *rows.shape)), "zh")
    got = swapped(jnp.broadcast_to(block, (8, *block.shape)), ("zl", "y"))
    got = got.reshape(2, NY, 4, *rows.shape)
    return jnp.transpose(got, (3, 2, 0, 1, 4, 5)).reshape(count, -1, width)


def gates(pre):
    sig = 1.0 / (1.0 + jnp.exp(-pre))
    d_sig = sig * (1.0 - sig)
    return pre * sig, sig + pre * d_sig, d_sig * (2.0 + pre * (1.0 - 2.0 * sig))


def attention_of(queries, keys, values, tail_k, tail_v, seq_index):
    tok_rows, head_dim = queries.shape
    key_all = jnp.concatenate([tail_k, keys], axis=0)
    value_all = jnp.concatenate([tail_v, values], axis=0)
    scores = lax.dot_general(
        queries, key_all, (((1,), (1,)), ((), ())), preferred_element_type=f32
    ) * head_dim ** (-0.5)
    query_pos = jnp.arange(tok_rows, dtype=jnp.int32)[:, None]
    key_pos = jnp.arange(tok_rows + WIN, dtype=jnp.int32)[None, :] - WIN
    in_window = (
        (key_pos <= query_pos)
        & (key_pos > query_pos - WIN)
        & (key_pos + seq_index * tok_rows >= 0)
    )
    scores = jnp.where(in_window, scores, -1e30)
    row_max = jnp.max(scores, axis=-1, keepdims=True)
    expo = jnp.exp(scores - row_max)
    probs = (expo / jnp.sum(expo, axis=-1, keepdims=True)).astype(bf16)
    return jnp.dot(probs, value_all, preferred_element_type=f32)


def row_scale(weights, updated):
    target = jnp.sqrt(jnp.mean(weights * weights, axis=-1, keepdims=True))
    return target / jnp.sqrt(jnp.mean(updated * updated, axis=-1, keepdims=True) + 1e-06)


def renorm(weights, updated):
    return updated * row_scale(weights, updated)


def adam_step(weights, gradient, first_moment, second_moment):
    first_next = beta_one * first_moment + (1.0 - beta_one) * gradient
    second_next = beta_two * second_moment + (1.0 - beta_two) * gradient * gradient
    first_hat = first_next / (1.0 - beta_one**10)
    second_hat = second_next / (1.0 - beta_two**10)
    return (
        weights - adam_rate * first_hat / (jnp.sqrt(second_hat) + 1e-08),
        first_next,
        second_next,
    )


def local(queries, keys, values, rates, gain, cotangent, fast_init, first_moment, second_moment):
    tok_rows, dim = queries.shape
    z = lax.axis_index(Z)
    y = lax.axis_index("y")
    seq_index = z * NY + y
    scale = dim ** (-0.5)
    weights = fast_init[0]

    last = NY * NZ - 1
    pairs = [(i, i + 1) for i in range(last)]
    tails = [lax.ppermute(a[tok_rows - WIN :], SEQ, pairs) for a in (keys, values)]

    first_pre = scale * mm(keys, weights[0], 1, 0)
    third_pre = scale * mm(keys, weights[1], 1, 0)
    gate, gate1, gate2 = gates(first_pre)
    factor = (-scale) * rates[0][:, None]
    err = factor * values.astype(f32)
    back = factor * mm(values, weights[2], 1, 0)
    grads = jnp.stack(
        [
        scale * mm(keys, back * third_pre * gate1, 0, 0),
        scale * mm(keys, back * gate, 0, 0),
        mm(err, gate * third_pre, 0, 0),
        ]
    )
    update_rows = reduce_rows(grads)
    rows = dim // (NY * NZ)
    init_rows = lax.dynamic_slice_in_dim(weights, seq_index * rows, rows, 1)
    moved_rows = init_rows - update_rows
    renormed = gather_rows(renorm(init_rows, moved_rows).astype(bf16))

    first_q = scale * mm(queries, renormed[0], 1, 0)
    third_q = scale * mm(queries, renormed[1], 1, 0)
    gate_q, gate1_q, _ = gates(first_q)
    hidden_q = gate_q * third_q
    fast_out = scale * mm(hidden_q, renormed[2], 1, 1)
    weighted = cotangent.astype(f32) * gain[None, :]
    sums = jnp.stack([jnp.sum(fast_out * fast_out, axis=1), jnp.sum(weighted * fast_out, axis=1)])
    sums = jnp.sum(swapped(jnp.broadcast_to(sums, (8, *sums.shape)), HEAD), axis=0)
    root = jnp.sqrt(sums[0] / WIDTH + 1e-06)[:, None]
    coef = sums[1][:, None] / (WIDTH * root**3)
    d_fast = weighted / root - fast_out * coef
    err_q = scale * d_fast
    back_q = mm(err_q, renormed[2], 1, 0)
    grads = jnp.stack(
        [
        scale * mm(queries, back_q * third_q * gate1_q, 0, 0),
        scale * mm(queries, back_q * gate_q, 0, 0),
        mm(err_q, hidden_q, 0, 0),
        ]
    )
    cot_rows = reduce_rows(grads)
    _, pull_norm = jax.vjp(renorm, init_rows, moved_rows)
    d_init_rows, d_moved_rows = pull_norm(cot_rows)
    local_part = d_init_rows + d_moved_rows
    direction = gather_rows(d_moved_rows.astype(bf16))

    first_dot = scale * mm(keys, direction[0], 1, 0)
    third_dot = scale * mm(keys, direction[1], 1, 0)
    back_dot = factor * mm(values, direction[2], 1, 0)
    bent = gate1 * first_dot
    grads = jnp.stack(
        [
        scale
        * mm(
            keys,
            back_dot * third_pre * gate1
            + back * third_dot * gate1
            + back * third_pre * gate2 * first_dot,
            0,
            0,
        ),
        scale * mm(keys, back_dot * gate + back * bent, 0, 0),
        mm(err, bent * third_pre + gate * third_dot, 0, 0),
        ]
    )
    grad_rows = local_part - reduce_rows(grads)

    attention = attention_of(queries, keys, values, tails[0], tails[1], seq_index)
    normed = fast_out / root * gain[None, :]
    layer_out = (attention + normed).astype(bf16)
    new = adam_step(init_rows, grad_rows, first_moment[0], second_moment[0])
    return (layer_out, new[0][None], new[1][None], new[2][None])


def solution(mesh):
    split = Mesh(mesh.devices.reshape(4, 2, NY, 4, 2), ("zh", "zl", "y", "x", "c"))
    placed = (
        P(SEQ, HEAD),
        P(SEQ, HEAD),
        P(SEQ, HEAD),
        P(HEAD, SEQ),
        P(HEAD),
        P(SEQ, HEAD),
        P(HEAD, None, None, None),
        P(HEAD, None, SEQ, None),
        P(HEAD, None, SEQ, None),
    )
    return jax.shard_map(
        local,
        mesh=split,
        in_specs=placed,
        out_specs=(
            P(SEQ, HEAD),
            P(HEAD, None, SEQ, None),
            P(HEAD, None, SEQ, None),
            P(HEAD, None, SEQ, None),
        ),
        check_vma=False,
    )
```

profile of v0, /device:TPU:24, one launch (start us, length us, event | category | flops | bytes accessed | tf_op | source)
XLA Modules:
  0.0 249.0 jit_solution(17118798964345153582)
XLA Ops:
  0.7 2.2 convert.50
  2.9 1.5 convolution_multiply_fusion.11
  4.4 1.4 convolution_multiply_fusion.12
  8.1 1.3 fusion.19
  9.9 1.4 fusion.20
  11.3 1.3 copy.153
  12.5 2.8 %convolution_convert_fusion.2 = bf16[512,512]{1,0:T(8,128)(2,1)} fusion(f32[512,512]{0,1:T(8,128)} %convolution_multiply_fusion.12, bf16[512,512]{0,1:T(8,128)(2,1)} %copy.156, f32[512]{0:T(512)S(1)} %bitcast.134, f32[512,512]{0,1:T(8,128)S(1)} %copy-done.11), kind=kOutput, calls=%fused_computation.34 | convolution fusion | flops 271056896 | bytes 3147776 | tf_op jit(solution)/shard_map/dot_general | solution.py:22
  17.9 23.1 %all_to_all.55 = bf16[4,3,8,16,512]{4,3,2,1,0:T(8,128)(2,1)S(1)} all-to-all(bf16[4,3,8,16,512]{4,3,2,1,0:T(8,128)(2,1)S(1)} %copy.157), channel_id=1, replica_groups=mesh['zh'=4,'zl'=2,'y'=4,'x'=4,'c'=2] {'y'}, dimensions={0} | all-to-all | bytes 3145728 | tf_op jit(solution)/shard_map/all_to_all | solution.py:28
  42.2 8.5 %all-to-all-start.1 = ((bf16[8,3,16,512]{3,2,1,0:T(8,128)(2,1)}), bf16[8,3,16,512]{3,2,1,0:T(8,128)(2,1)S(1)}, u32[]{:S(2)}, u32[]{:S(2)}) async-start(bf16[8,3,16,512]{3,2,1,0:T(8,128)(2,1)} %copy.158), calls=%async_computation.1 | async-start | bytes 786432 | tf_op jit(solution)/shard_map/all_to_all | solution.py:28
  50.6 13.6 %all-to-all-done.1 = bf16[8,3,16,512]{3,2,1,0:T(8,128)(2,1)S(1)} async-done(((bf16[8,3,16,512]{3,2,1,0:T(8,128)(2,1)}), bf16[8,3,16,512]{3,2,1,0:T(8,128)(2,1)S(1)}, u32[]{:S(2)}, u32[]{:S(2)}) %all-to-all-start.1) | async-done | bytes 393248 | tf_op jit(solution)/shard_map/all_to_all | solution.py:28
  65.4 11.6 %all_to_all.56 = bf16[4,3,16,512]{3,2,1,0:T(8,128)(2,1)S(1)} all-to-all(bf16[4,3,16,512]{3,2,1,0:T(8,128)(2,1)S(1)} %broadcast_in_dim.23), channel_id=1, replica_groups=mesh['zh'=4,'zl'=2,'y'=4,'x'=4,'c'=2] {'zh'}, dimensions={0} | all-to-all | bytes 393216 | tf_op jit(solution)/shard_map/all_to_all | solution.py:28
  77.2 20.0 %all_to_all.57 = bf16[8,4,3,16,512]{4,3,1,2,0:T(8,128)(2,1)S(1)} all-to-all(bf16[8,4,3,16,512]{4,3,1,2,0:T(8,128)(2,1)S(1)} %broadcast_in_dim.46), channel_id=1, replica_groups=mesh['zh'=4,'zl'=2,'y'=4,'x'=4,'c'=2] {'zl','y'}, dimensions={0} | all-to-all | bytes 3145728 | tf_op jit(solution)/shard_map/all_to_all | solution.py:28
  98.1 1.5 multiply_convert_fusion.2
  100.4 9.5 %all_to_all.58 = f32[8,2,512]{2,1,0:T(2,128)S(1)} all-to-all(f32[8,2,512]{2,1,0:T(2,128)S(1)} %broadcast_in_dim.47), channel_id=1, replica_groups=mesh['zh'=4,'zl'=2,'y'=4,'x'=4,'c'=2] {'x','c'}, dimensions={0} | all-to-all | bytes 65536 | tf_op jit(solution)/shard_map/all_to_all | solution.py:28
  110.0 1.3 multiply_convert_fusion.1
  112.9 1.3 fusion.17
  115.0 1.3 copy.169
  116.6 23.7 %all_to_all.59 = bf16[4,3,8,16,512]{4,3,2,1,0:T(8,128)(2,1)S(1)} all-to-all(bf16[4,3,8,16,512]{4,3,2,1,0:T(8,128)(2,1)S(1)} %copy.170), channel_id=1, replica_groups=mesh['zh'=4,'zl'=2,'y'=4,'x'=4,'c'=2] {'y'}, dimensions={0} | all-to-all | bytes 3145728 | tf_op jit(solution)/shard_map/all_to_all | solution.py:28
  140.7 16.1 %all_to_all.60 = bf16[8,3,16,512]{3,2,1,0:T(8,128)(2,1)S(1)} all-to-all(bf16[8,3,16,512]{3,2,1,0:T(8,128)(2,1)S(1)} %copy.171), channel_id=1, replica_groups=mesh['zh'=4,'zl'=2,'y'=4,'x'=4,'c'=2] {'zh','zl'}, dimensions={0} | all-to-all | bytes 786432 | tf_op jit(solution)/shard_map/all_to_all | solution.py:28
  157.1 11.6 %all_to_all.61 = bf16[4,3,16,512]{3,2,1,0:T(8,128)(2,1)S(1)} all-to-all(bf16[4,3,16,512]{3,2,1,0:T(8,128)(2,1)S(1)} %broadcast_in_dim.52), channel_id=1, replica_groups=mesh['zh'=4,'zl'=2,'y'=4,'x'=4,'c'=2] {'zh'}, dimensions={0} | all-to-all | bytes 393216 | tf_op jit(solution)/shard_map/all_to_all | solution.py:28
  168.9 20.8 %all_to_all.62 = bf16[8,4,3,16,512]{4,3,1,2,0:T(8,128)(2,1)S(1)} all-to-all(bf16[8,4,3,16,512]{4,3,1,2,0:T(8,128)(2,1)S(1)} %broadcast_in_dim.53), channel_id=1, replica_groups=mesh['zh'=4,'zl'=2,'y'=4,'x'=4,'c'=2] {'zl','y'}, dimensions={0} | all-to-all | bytes 3145728 | tf_op jit(solution)/shard_map/all_to_all | solution.py:28
  194.9 1.7 convolution_convert_fusion
  198.2 1.3 copy.178
  199.5 6.0 %all-to-all-start.9 = ((bf16[4,3,8,16,512]{4,3,2,1,0:T(8,128)(2,1)}), bf16[4,3,8,16,512]{4,3,2,1,0:T(8,128)(2,1)S(1)}, u32[]{:S(2)}, u32[]{:S(2)}) async-start(bf16[4,3,8,16,512]{4,3,2,1,0:T(8,128)(2,1)} %copy.178), calls=%async_computation.9 | async-start | bytes 3145728 | tf_op jit(solution)/shard_map/all_to_all | solution.py:28
  206.2 2.0 collective-permute-start
  208.2 3.9 %collective-permute-start.1 = (bf16[256,512]{1,0:T(8,128)(2,1)S(1)}, bf16[256,512]{1,0:T(8,128)(2,1)}, u32[]{:S(2)}, u32[]{:S(2)}) collective-permute-start(bf16[256,512]{1,0:T(8,128)(2,1)S(1)} %slice.53), channel_id=1, source_target_pairs={{0,8},{8,16},{16,24},{24,32},{32,40},{40,48},{48,56},{56,64},{64,7... | collective-permute-start | bytes 786440 | tf_op jit(solution)/shard_map/ppermute | solution.py:106
  212.1 15.7 %collective-permute-done = bf16[256,512]{1,0:T(8,128)(2,1)} collective-permute-done((bf16[256,512]{1,0:T(8,128)(2,1)}, bf16[256,512]{1,0:T(8,128)(2,1)}, u32[]{:S(2)}, u32[]{:S(2)}) %collective-permute-start) | collective-permute-done | bytes 262176 | tf_op jit(solution)/shard_map/ppermute | solution.py:106
  227.8 3.0 %fusion.69 = (f32[512]{0:T(512)S(1)}, f32[512,768]{0,1:T(8,128)}) fusion(bf16[512,512]{1,0:T(8,128)(2,1)S(1)} %copy-done, bf16[512,512]{1,0:T(8,128)(2,1)S(1)} %copy-done.1, bf16[256,512]{1,0:T(8,128)(2,1)} %collective-permute-done, pred[768]{0:T(1024)(128)(4,1)S(1)} %add_compare_fusion, s32[512]{0:T(512)S(1)} %iota_add_fusion.1, s32[768]{0:T(1024)S(1)} %iota_add_fusion), kind=kOutput, calls=%fused_computation.134 | convolution fusion | flops 406978048 | bytes 2891520 | tf_op jit(solution)/shard_map/dot_general | solution.py:58
  231.9 3.5 %all-to-all-start.10 = ((bf16[8,3,16,512]{3,2,1,0:T(8,128)(2,1)}), bf16[8,3,16,512]{3,2,1,0:T(8,128)(2,1)S(1)}, u32[]{:S(2)}, u32[]{:S(2)}) async-start(bf16[8,3,16,512]{3,2,1,0:T(8,128)(2,1)} %copy.179), calls=%async_computation.10 | async-start | bytes 786432 | tf_op jit(solution)/shard_map/all_to_all | solution.py:28
  236.6 2.4 fusion.8
  239.0 8.2 %all-to-all-done.10 = bf16[8,3,16,512]{3,2,1,0:T(8,128)(2,1)S(1)} async-done(((bf16[8,3,16,512]{3,2,1,0:T(8,128)(2,1)}), bf16[8,3,16,512]{3,2,1,0:T(8,128)(2,1)S(1)}, u32[]{:S(2)}, u32[]{:S(2)}) %all-to-all-start.10) | async-done | bytes 393248 | tf_op jit(solution)/shard_map/all_to_all | solution.py:28
  247.2 1.8 divide_subtract_fusion
  (122 shorter events, 22.8 us)
Async XLA Ops:
  0.6 96.9 %copy-start = (bf16[512,512]{1,0:T(8,128)(2,1)S(1)}, bf16[512,512]{1,0:T(8,128)(2,1)}, u32[]{:S(2)}) copy-start(bf16[512,512]{1,0:T(8,128)(2,1)} %param.9) | copy-start | bytes 1572868
  0.6 2.2 copy-start.1
  2.8 3.0 %copy-start.29 = (f32[1,512]{1,0:T(1,128)S(1)}, f32[1,512]{1,0:T(1,128)}, u32[]{:S(2)}) copy-start(f32[1,512]{1,0:T(1,128)} %param.12) | copy-start | bytes 6148
  4.4 1.5 copy-start.2
  6.9 1.2 copy-start.10
  8.1 1.3 copy-start.6
  8.1 1.8 copy-start.13
  9.9 2.6 %copy-start.11 = (f32[512,512]{0,1:T(8,128)S(1)}, f32[512,512]{0,1:T(8,128)}, u32[]{:S(2)}) copy-start(f32[512,512]{0,1:T(8,128)} %convolution_multiply_fusion.11) | copy-start | bytes 3145732
  42.2 22.0 %all-to-all-start.1 = ((bf16[8,3,16,512]{3,2,1,0:T(8,128)(2,1)}), bf16[8,3,16,512]{3,2,1,0:T(8,128)(2,1)S(1)}, u32[]{:S(2)}, u32[]{:S(2)}) async-start(bf16[8,3,16,512]{3,2,1,0:T(8,128)(2,1)} %copy.158), calls=%async_computation.1 | async-start | bytes 786432 | tf_op jit(solution)/shard_map/all_to_all | solution.py:28
  64.2 12.8 %copy-start.17 = (f32[3,16,512]{2,1,0:T(8,128)}, f32[3,16,512]{2,1,0:T(8,128)S(1)}, u32[]{:S(2)}) copy-start(f32[3,16,512]{2,1,0:T(8,128)S(1)} %convert_reduce_fusion.2) | copy-start | bytes 294916
  65.3 11.8 %copy-start.4 = (f32[3,16,512]{2,1,0:T(8,128)}, f32[3,16,512]{2,1,0:T(8,128)S(1)}, u32[]{:S(2)}) copy-start(f32[3,16,512]{2,1,0:T(8,128)S(1)} %get-tuple-element.10) | copy-start | bytes 294916
  98.0 1.6 copy-start.15
  98.0 1.6 copy-start.19
  98.1 1.5 copy-start.27
  100.3 11.6 %copy-start.8 = (f32[512,512]{1,0:T(8,128)}, f32[512,512]{1,0:T(8,128)S(1)}, u32[]{:S(2)}) copy-start(f32[512,512]{1,0:T(8,128)S(1)} %get-tuple-element.26) | copy-start | bytes 3145732
  110.0 1.9 copy-start.25
  111.3 1.5 copy-start.16
  112.9 1.3 copy-start.30
  140.6 16.2 %copy-start.5 = (f32[3,16,512]{2,1,0:T(8,128)S(1)}, f32[3,16,512]{2,1,0:T(8,128)}, u32[]{:S(2)}) copy-start(f32[3,16,512]{2,1,0:T(8,128)} %copy-done.4) | copy-start | bytes 294916
  191.1 1.2 copy-start.7
  191.1 1.5 copy-start.12
  199.5 31.2 %all-to-all-start.9 = ((bf16[4,3,8,16,512]{4,3,2,1,0:T(8,128)(2,1)}), bf16[4,3,8,16,512]{4,3,2,1,0:T(8,128)(2,1)S(1)}, u32[]{:S(2)}, u32[]{:S(2)}) async-start(bf16[4,3,8,16,512]{4,3,2,1,0:T(8,128)(2,1)} %copy.178), calls=%async_computation.9 | async-start | bytes 3145728 | tf_op jit(solution)/shard_map/all_to_all | solution.py:28
  206.2 21.6 %collective-permute-start = (bf16[256,512]{1,0:T(8,128)(2,1)}, bf16[256,512]{1,0:T(8,128)(2,1)}, u32[]{:S(2)}, u32[]{:S(2)}) collective-permute-start(bf16[256,512]{1,0:T(8,128)(2,1)} %slice.52), channel_id=1, source_target_pairs={{0,8},{8,16},{16,24},{24,32},{32,40},{40,48},{48,56},{56,64},{64,7... | collective-permute-start | bytes 786440 | tf_op jit(solution)/shard_map/ppermute | solution.py:106
  208.2 27.5 %collective-permute-start.1 = (bf16[256,512]{1,0:T(8,128)(2,1)S(1)}, bf16[256,512]{1,0:T(8,128)(2,1)}, u32[]{:S(2)}, u32[]{:S(2)}) collective-permute-start(bf16[256,512]{1,0:T(8,128)(2,1)S(1)} %slice.53), channel_id=1, source_target_pairs={{0,8},{8,16},{16,24},{24,32},{32,40},{40,48},{48,56},{56,64},{64,7... | collective-permute-start | bytes 786440 | tf_op jit(solution)/shard_map/ppermute | solution.py:106
  231.1 4.3 %copy-start.3 = (f32[512,768]{0,1:T(8,128)S(1)}, f32[512,768]{0,1:T(8,128)}, u32[]{:S(2)}) copy-start(f32[512,768]{0,1:T(8,128)} %get-tuple-element.25) | copy-start | bytes 4718596
  231.1 4.6 %copy-start.26 = (f32[1,512]{1,0:T(1,128)S(1)}, f32[1,512]{1,0:T(1,128)}, u32[]{:S(2)}) copy-start(f32[1,512]{1,0:T(1,128)} %copy-done.25) | copy-start | bytes 6148
  231.1 4.6 %copy-start.28 = (f32[512]{0:T(512)S(1)}, f32[512]{0:T(512)}, u32[]{:S(2)}) copy-start(f32[512]{0:T(512)} %param.13) | copy-start | bytes 6148
  231.9 15.3 %all-to-all-start.10 = ((bf16[8,3,16,512]{3,2,1,0:T(8,128)(2,1)}), bf16[8,3,16,512]{3,2,1,0:T(8,128)(2,1)S(1)}, u32[]{:S(2)}, u32[]{:S(2)}) async-start(bf16[8,3,16,512]{3,2,1,0:T(8,128)(2,1)} %copy.179), calls=%async_computation.10 | async-start | bytes 786432 | tf_op jit(solution)/shard_map/all_to_all | solution.py:28
  235.4 1.2 copy-start.9
  235.7 11.6 %copy-start.18 = (f32[3,16,512]{2,1,0:T(8,128)S(1)}, f32[3,16,512]{2,1,0:T(8,128)}, u32[]{:S(2)}) copy-start(f32[3,16,512]{2,1,0:T(8,128)} %copy-done.17) | copy-start | bytes 294916
  236.6 10.6 %copy-start.23 = (f32[1,3,16,512]{3,2,1,0:T(8,128)S(1)}, f32[1,3,16,512]{3,2,1,0:T(8,128)}, u32[]{:S(2)}) copy-start(f32[1,3,16,512]{3,2,1,0:T(8,128)} %param.16) | copy-start | bytes 294916
  236.6 10.7 %copy-start.24 = (f32[1,3,16,512]{3,2,1,0:T(8,128)S(1)}, f32[1,3,16,512]{3,2,1,0:T(8,128)}, u32[]{:S(2)}) copy-start(f32[1,3,16,512]{3,2,1,0:T(8,128)} %param.17) | copy-start | bytes 294916
  (4 other events, 4.1 us)
where the time goes:
time: 250 us; the launch traced here: 249 us
  blocking collectives  137 us (55%)
  waiting for transfers between devices  37.4 us (15%)
  matrix products  24.7 us (10%)
  starting transfers between devices  23.7 us (9%)
  local copies, waits for them, and re-layouts  14.8 us (6%)
  other arithmetic  10.7 us (4%)
    all_to_all x8, blocking collectives, swapped(): return lax.all_to_all(parts, axes, split_axis=0, concat_axis=0, tiled=True)  137 us
    all_to_all x3, waiting for transfers between devices, swapped(): return lax.all_to_all(parts, axes, split_axis=0, concat_axis=0, tiled=True)  21.7 us
    dot_general x19, matrix products, mm(): lax.dot_general(a.astype(bf16), b.astype(bf16), (((ca,), (cb,)), ((), ())...  19.3 us
    all_to_all x3, starting transfers between devices, swapped(): return lax.all_to_all(parts, axes, split_axis=0, concat_axis=0, tiled=True)  17.9 us
    ppermute x2, waiting for transfers between devices, local(): lax.ppermute(a[tok_rows - WIN:], SEQ, pairs)  15.7 us
    ppermute x2, starting transfers between devices, local(): lax.ppermute(a[tok_rows - WIN:], SEQ, pairs)  5.86 us
    unnamed x63, local copies, waits for them, and re-layouts  5.42 us
  transfers between devices with their start and end apart: 5, of which 3 were waited for; matrix products, arithmetic and copies ran while one was open for 3% of the time, Pallas kernels for 0%

commit v1 on v0

v1 whole, which is shorter than its diff:
```python
import jax
import jax.numpy as jnp
from jax import lax
from jax.experimental import pallas as pl
from jax.experimental.pallas import tpu as pltpu
from jax.sharding import Mesh
from jax.sharding import PartitionSpec as P

WIN = 256
WIDTH = 4096
SEQ = ("zh", "zl", "y")
PLANE = ("zl", "y")
HEAD = ("x", "c")
NY = 4
NH = 4
NP = 8
ROWS = 16
BLOCK = 128
beta_one = 0.9
beta_two = 0.95
adam_rate = 0.02
bf16 = jnp.bfloat16
f32 = jnp.float32


def mm(a, b, ca, cb):
    return lax.dot_general(
        a.astype(bf16), b.astype(bf16), (((ca,), (cb,)), ((), ())), preferred_element_type=f32
    )


def swapped(parts, axes):
    return lax.all_to_all(parts, axes, split_axis=0, concat_axis=0, tiled=True)


def copies(array, count):
    return jnp.broadcast_to(array, (count, *array.shape))


def totals(parts):
    return jnp.sum(parts.astype(f32), axis=0)


def gates(pre):
    sig = 1.0 / (1.0 + jnp.exp(-pre))
    d_sig = sig * (1.0 - sig)
    return pre * sig, sig + pre * d_sig, d_sig * (2.0 + pre * (1.0 - 2.0 * sig))


def columns(row):
    return jnp.broadcast_to(row, (128, row.shape[1])).T


def line(col):
    return jnp.broadcast_to(col, (col.shape[0], 128)).T[:1, :]


def blocks_of(count, body):
    def step(j, carry):
        body(pl.ds(pl.multiple_of(j * BLOCK, BLOCK), BLOCK))
        return carry

    lax.fori_loop(0, count // BLOCK, step, 0)


def put_grad(parts_ref, number, left, right):
    grad = mm(left[...], right[...], 0, 0).astype(bf16)
    for m in range(grad.shape[0] // ROWS):
        parts_ref[m % NP, number, m // NP] = grad[m * ROWS : (m + 1) * ROWS]


def take_matrices(parts_ref, out_ref):
    for number in range(out_ref.shape[0]):
        for m in range(out_ref.shape[1] // ROWS):
            out_ref[number, m * ROWS : (m + 1) * ROWS, :] = parts_ref[m % NP, number, m // NP]


def inner_kernel(k_ref, v_ref, r_ref, w_ref, parts_ref, p1_ref, p3_ref, b_ref, w_s, f_s, d1, d3, d2):
    tokens, dim = k_ref.shape
    scale = dim ** (-0.5)
    for m in range(3):
        w_s[m] = w_ref[m].astype(bf16)
    f_s[...] = columns(r_ref[...] * (-scale))

    def body(at):
        factor = f_s[at, :][:, :1]
        p1 = scale * mm(k_ref[at, :], w_s[0], 1, 0)
        p3 = scale * mm(k_ref[at, :], w_s[1], 1, 0)
        back = factor * mm(v_ref[at, :], w_s[2], 1, 0)
        gate, gate1, _ = gates(p1)
        p1_ref[at, :] = p1
        p3_ref[at, :] = p3
        b_ref[at, :] = back
        d1[at, :] = (scale * back * p3 * gate1).astype(bf16)
        d3[at, :] = (scale * back * gate).astype(bf16)
        d2[at, :] = (factor * gate * p3).astype(bf16)

    blocks_of(tokens, body)
    put_grad(parts_ref, 0, k_ref, d1)
    put_grad(parts_ref, 1, k_ref, d3)
    put_grad(parts_ref, 2, v_ref, d2)


def forward_kernel(got_ref, q_ref, cot_ref, gain_ref, o_ref, p1_ref, p3_ref, sums_ref, w2_ref, w_s, s_s):
    tokens, dim = q_ref.shape
    scale = dim ** (-0.5)
    take_matrices(got_ref, w_s)
    w2_ref[...] = w_s[2]

    def body(at):
        p1 = scale * mm(q_ref[at, :], w_s[0], 1, 0)
        p3 = scale * mm(q_ref[at, :], w_s[1], 1, 0)
        gate, _, _ = gates(p1)
        out = scale * mm(gate * p3, w_s[2], 1, 1)
        p1_ref[at, :] = p1
        p3_ref[at, :] = p3
        o_ref[at, :] = out
        weighted = cot_ref[at, :].astype(f32) * gain_ref[...]
        squares = jnp.sum(out * out, axis=1, keepdims=True)
        inner = jnp.sum(weighted * out, axis=1, keepdims=True)
        lane = lax.broadcasted_iota(jnp.int32, (BLOCK, 128), 1)
        s_s[at, :] = jnp.where(lane == 0, squares, inner)

    blocks_of(tokens, body)
    sums_ref[...] = jnp.broadcast_to(s_s[...].T[:2, :], sums_ref.shape)


def backward_kernel(
    sums_ref, o_ref, p1_ref, p3_ref, q_ref, cot_ref, gain_ref, w2_ref,
    parts_ref, normed_ref, s_s, d1, d3, a_s, e_s,
):
    tokens, dim = q_ref.shape
    scale = dim ** (-0.5)
    sums = jnp.sum(sums_ref[...], axis=0)
    inverse = 1.0 / jnp.sqrt(sums[:1] / WIDTH + 1e-06)
    coef = sums[1:] * inverse * inverse * inverse / WIDTH
    s_s[0] = columns(inverse)
    s_s[1] = columns(coef)

    def body(at):
        inv = s_s[0, at, :][:, :1]
        out = o_ref[at, :]
        weighted = cot_ref[at, :].astype(f32) * gain_ref[...]
        err = (scale * (weighted * inv - out * s_s[1, at, :][:, :1])).astype(bf16)
        e_s[at, :] = err
        normed_ref[at, :] = out * inv * gain_ref[...]
        back = mm(err, w2_ref[...], 1, 0)
        p3 = p3_ref[at, :]
        gate, gate1, _ = gates(p1_ref[at, :])
        d1[at, :] = (scale * back * p3 * gate1).astype(bf16)
        d3[at, :] = (scale * back * gate).astype(bf16)
        a_s[at, :] = (gate * p3).astype(bf16)

    blocks_of(tokens, body)
    put_grad(parts_ref, 0, q_ref, d1)
    put_grad(parts_ref, 1, q_ref, d3)
    put_grad(parts_ref, 2, e_s, a_s)


def second_kernel(got_ref, k_ref, v_ref, r_ref, p1_ref, p3_ref, b_ref, parts_ref, w_s, f_s, d1, d3, d2):
    tokens, dim = k_ref.shape
    scale = dim ** (-0.5)
    take_matrices(got_ref, w_s)
    f_s[...] = columns(r_ref[...] * (-scale))

    def body(at):
        factor = f_s[at, :][:, :1]
        first_dot = scale * mm(k_ref[at, :], w_s[0], 1, 0)
        third_dot = scale * mm(k_ref[at, :], w_s[1], 1, 0)
        back_dot = factor * mm(v_ref[at, :], w_s[2], 1, 0)
        p3 = p3_ref[at, :]
        back = b_ref[at, :]
        gate, gate1, gate2 = gates(p1_ref[at, :])
        bent = gate1 * first_dot
        d1[at, :] = (
            scale
            * (gate1 * (back_dot * p3 + back * third_dot) + back * p3 * gate2 * first_dot)
        ).astype(bf16)
        d3[at, :] = (scale * (back_dot * gate + back * bent)).astype(bf16)
        d2[at, :] = (factor * (bent * p3 + gate * third_dot)).astype(bf16)

    blocks_of(tokens, body)
    put_grad(parts_ref, 0, k_ref, d1)
    put_grad(parts_ref, 1, k_ref, d3)
    put_grad(parts_ref, 2, v_ref, d2)


def called(kernel, outs, scratch, *args):
    return pl.pallas_call(
        kernel,
        out_shape=[jax.ShapeDtypeStruct(*out) for out in outs],
        in_specs=[pl.BlockSpec(memory_space=pltpu.VMEM)] * len(args),
        out_specs=[pl.BlockSpec(memory_space=pltpu.VMEM)] * len(outs),
        scratch_shapes=[pltpu.VMEM(*item) for item in scratch],
    )(*args)


def to_owners(parts):
    return totals(swapped(parts, PLANE)).astype(bf16)


def attention_of(queries, keys, values, tail_k, tail_v, seq_index):
    tok_rows, head_dim = queries.shape
    key_all = jnp.concatenate([tail_k, keys], axis=0)
    value_all = jnp.concatenate([tail_v, values], axis=0)
    scores = lax.dot_general(
        queries, key_all, (((1,), (1,)), ((), ())), preferred_element_type=f32
    ) * head_dim ** (-0.5)
    query_pos = jnp.arange(tok_rows, dtype=jnp.int32)[:, None]
    key_pos = jnp.arange(tok_rows + WIN, dtype=jnp.int32)[None, :] - WIN
    in_window = (
        (key_pos <= query_pos)
        & (key_pos > query_pos - WIN)
        & (key_pos + seq_index * tok_rows >= 0)
    )
    scores = jnp.where(in_window, scores, -1e30)
    row_max = jnp.max(scores, axis=-1, keepdims=True)
    expo = jnp.exp(scores - row_max)
    probs = (expo / jnp.sum(expo, axis=-1, keepdims=True)).astype(bf16)
    return jnp.dot(probs, value_all, preferred_element_type=f32)


def renorm(weights, updated):
    target = jnp.sqrt(jnp.mean(weights * weights, axis=-1, keepdims=True))
    return updated * (
        target / jnp.sqrt(jnp.mean(updated * updated, axis=-1, keepdims=True) + 1e-06)
    )


def adam_step(weights, gradient, first_moment, second_moment):
    first_next = beta_one * first_moment + (1.0 - beta_one) * gradient
    second_next = beta_two * second_moment + (1.0 - beta_two) * gradient * gradient
    first_hat = first_next / (1.0 - beta_one**10)
    second_hat = second_next / (1.0 - beta_two**10)
    return (
        weights - adam_rate * first_hat / (jnp.sqrt(second_hat) + 1e-08),
        first_next,
        second_next,
    )


def local(queries, keys, values, rates, gain, cotangent, fast_init, first_moment, second_moment):
    tokens, dim = queries.shape
    zh = lax.axis_index("zh")
    plane = lax.axis_index(PLANE)
    weights = fast_init[0]
    full, half = ((tokens, dim), f32), ((tokens, dim), bf16)
    side = ((tokens, 128), f32)
    mats = ((3, dim, dim), bf16)
    owned = ((NP, 3, NH, ROWS, dim), bf16)
    gain_row = gain[None, :]

    last = NY * NP - 1
    pairs = [(i, i + 1) for i in range(last)]
    tails = [lax.ppermute(a[tokens - WIN :], SEQ, pairs) for a in (keys, values)]

    parts, first_pre, third_pre, back = called(
        inner_kernel, [owned, full, full, full], [mats, side, half, half, half],
        keys, values, rates, weights,
    )
    init_rows = lax.dynamic_index_in_dim(
        weights.reshape(3, NH, NP, ROWS, dim), plane, 2, keepdims=False
    )
    moved_rows = init_rows - totals(swapped(copies(to_owners(parts), NH), "zh"))
    rows = renorm(init_rows, moved_rows).astype(bf16)
    renormed = swapped(copies(rows, NP), PLANE)

    fast_out, first_q, third_q, sums, second_w = called(
        forward_kernel, [full, full, full, ((NP, 2, tokens), f32), half], [mats, side],
        renormed, queries, cotangent, gain_row,
    )
    sums = swapped(sums, HEAD)
    parts, normed = called(
        backward_kernel, [owned, full], [((2, tokens, 128), f32), half, half, half, half],
        sums, fast_out, first_q, third_q, queries, cotangent, gain_row, second_w,
    )
    cot_rows = totals(swapped(copies(to_owners(parts), NH), "zh"))
    _, pull_norm = jax.vjp(renorm, init_rows, moved_rows)
    d_init_rows, d_moved_rows = pull_norm(cot_rows)
    direction = swapped(copies(d_moved_rows.astype(bf16), NP), PLANE)

    (parts,) = called(
        second_kernel, [owned], [mats, side, half, half, half],
        direction, keys, values, rates, first_pre, third_pre, back,
    )
    second_terms = totals(swapped(jnp.moveaxis(to_owners(parts), 1, 0), "zh"))

    def own(array):
        return lax.dynamic_index_in_dim(array, zh, 1, keepdims=False)

    grad_rows = own(d_init_rows + d_moved_rows) - second_terms
    attention = attention_of(
        queries, keys, values, tails[0], tails[1], zh * NP + plane
    )
    layer_out = (attention + normed).astype(bf16)
    new = adam_step(own(init_rows), grad_rows, first_moment[0], second_moment[0])
    return (layer_out, new[0][None], new[1][None], new[2][None])


def solution(mesh):
    split = Mesh(mesh.devices.reshape(NH, 2, NY, 4, 2), ("zh", "zl", "y", "x", "c"))
    placed = (
        P(SEQ, HEAD),
        P(SEQ, HEAD),
        P(SEQ, HEAD),
        P(HEAD, SEQ),
        P(HEAD),
        P(SEQ, HEAD),
        P(HEAD, None, None, None),
        P(HEAD, None, SEQ, None),
        P(HEAD, None, SEQ, None),
    )
    return jax.shard_map(
        local,
        mesh=split,
        in_specs=placed,
        out_specs=(
            P(SEQ, HEAD),
            P(HEAD, None, SEQ, None),
            P(HEAD, None, SEQ, None),
            P(HEAD, None, SEQ, None),
        ),
        check_vma=False,
    )
```

time: 250 us -> 243 us (0.972)
  Pallas kernels: 0 us -> 25.8 us
  matrix products: 24.7 us -> 5.04 us
  local copies, waits for them, and re-layouts: 14.8 us -> 4.74 us
  starting transfers between devices: 23.7 us -> 29.8 us
  other arithmetic: 10.7 us -> 5.63 us
  blocking collectives: 137 us -> 133 us
    pallas_call x0 -> x4, Pallas kernels: none -> 25.8 us  [called(): pl.pallas_call(kernel, out_shape=[jax.ShapeDtypeStruct(*out) for out in o...]
    dot_general x19 -> x0, matrix products: 19.3 us -> none  [mm(): lax.dot_general(a.astype(bf16), b.astype(bf16), (((ca,), (cb,)), ((), ())...]
    all_to_all x3, starting transfers between devices: 17.9 us -> 23.1 us  [swapped(): return lax.all_to_all(parts, axes, split_axis=0, concat_axis=0, tiled=True)]
    mul x6 -> x0, local copies, waits for them, and re-layouts: 4.39 us -> none  [the longest x1 1.25 us: local(): scale * mm(queries, back_q * gate_q, 0, 0)]
    unnamed x63 -> x12, local copies, waits for them, and re-layouts: 5.42 us -> 1.18 us
    all_to_all x8 -> x6, blocking collectives: 137 us -> 133 us  [swapped(): return lax.all_to_all(parts, axes, split_axis=0, concat_axis=0, tiled=True)]
    transpose x3 -> x0, other arithmetic: 2.61 us -> none  [reduce_rows(): got = swapped(jnp.transpose(blocks, (2, 0, 1, 3, 4)), 'y')]
where the time goes in v1:
time: 243 us
  blocking collectives  133 us (55%)
  waiting for transfers between devices  37.9 us (16%)
  starting transfers between devices  29.8 us (12%)
  Pallas kernels  25.8 us (11%)
  other arithmetic  5.63 us (2%)
  matrix products  5.04 us (2%)
  local copies, waits for them, and re-layouts  4.74 us (2%)
    all_to_all x6, blocking collectives, swapped(): return lax.all_to_all(parts, axes, split_axis=0, concat_axis=0, tiled=True)  133 us
    pallas_call x4, Pallas kernels, called(): pl.pallas_call(kernel, out_shape=[jax.ShapeDtypeStruct(*out) for out in o...  25.8 us
    all_to_all x3, starting transfers between devices, swapped(): return lax.all_to_all(parts, axes, split_axis=0, concat_axis=0, tiled=True)  23.1 us
    all_to_all x3, waiting for transfers between devices, swapped(): return lax.all_to_all(parts, axes, split_axis=0, concat_axis=0, tiled=True)  22.8 us
    ppermute x2, waiting for transfers between devices, local(): tails = [lax.ppermute(a[tokens - WIN:], SEQ, pairs) for a in (keys, values)]  15 us
    ppermute x2, starting transfers between devices, local(): tails = [lax.ppermute(a[tokens - WIN:], SEQ, pairs) for a in (keys, values)]  6.73 us
  transfers between devices with their start and end apart: 5, of which 3 were waited for; matrix products, arithmetic and copies ran while one was open for 3% of the time, Pallas kernels for 0%

profile of v1, /device:TPU:24, one launch (start us, length us, event | category | flops | bytes accessed | tf_op | source)
XLA Modules:
  0.0 242.6 jit_solution(7318065175473604404)
XLA Ops:
  0.6 6.4 %shard_map.120 = (bf16[8,3,4,16,512]{4,3,2,1,0:T(8,128)(2,1)}, f32[512,512]{1,0:T(8,128)}, f32[512,512]{1,0:T(8,128)}, f32[512,512]{1,0:T(8,128)}) custom-call(bf16[512,512]{1,0:T(8,128)(2,1)} %k_ref.3, bf16[512,512]{1,0:T(8,128)(2,1)} %v_ref.3, f32[1,512]{1,0:T(1,128)} %r_ref.3, f32[3,512,512]{2,1,0:T(8,128)} %bitcast.22), custom_call_target="tpu_custom_call" | custom-call | tf_op jit(solution)/shard_map/pallas_call | solution.py:189
  7.0 25.1 %all_to_all.45 = bf16[8,3,4,16,512]{4,3,2,1,0:T(8,128)(2,1)S(1)} all-to-all(bf16[8,3,4,16,512]{4,3,2,1,0:T(8,128)(2,1)} %get-tuple-element.15), channel_id=1, replica_groups=mesh['zh'=4,'zl'=2,'y'=4,'x'=4,'c'=2] {'zl','y'}, dimensions={0} | all-to-all | bytes 3145728 | tf_op jit(solution)/shard_map/all_to_all | solution.py:33
  32.1 0.3 reduce_sum.118
  32.4 1.0 broadcast_in_dim.40
  33.4 7.6 %all-to-all-start.1 = ((bf16[4,3,4,16,512]{4,3,2,1,0:T(8,128)(2,1)}), bf16[4,3,4,16,512]{4,3,2,1,0:T(8,128)(2,1)S(1)}, u32[]{:S(2)}, u32[]{:S(2)}) async-start(bf16[4,3,4,16,512]{4,3,2,1,0:T(8,128)(2,1)} %broadcast_in_dim.40), calls=%async_computation.1 | async-start | bytes 1572864 | tf_op jit(solution)/shard_map/all_to_all | solution.py:33
  41.0 17.4 %all-to-all-done.1 = bf16[4,3,4,16,512]{4,3,2,1,0:T(8,128)(2,1)S(1)} async-done(((bf16[4,3,4,16,512]{4,3,2,1,0:T(8,128)(2,1)}), bf16[4,3,4,16,512]{4,3,2,1,0:T(8,128)(2,1)S(1)}, u32[]{:S(2)}, u32[]{:S(2)}) %all-to-all-start.1) | async-done | bytes 786464 | tf_op jit(solution)/shard_map/all_to_all | solution.py:33
  58.5 1.1 multiply_reduce_fusion.1
  60.0 26.4 %all_to_all.46.got_ref = bf16[8,3,4,16,512]{4,3,2,1,0:T(8,128)(2,1)} all-to-all(bf16[8,3,4,16,512]{4,3,2,1,0:T(8,128)(2,1)S(1)} %broadcast_in_dim.41), channel_id=1, replica_groups=mesh['zh'=4,'zl'=2,'y'=4,'x'=4,'c'=2] {'zl','y'}, dimensions={0} | all-to-all | bytes 3145728 | tf_op jit(solution)/shard_map/all_to_all | solution.py:33
  86.5 5.8 %shard_map.121 = (f32[512,512]{1,0:T(8,128)}, f32[512,512]{1,0:T(8,128)}, f32[512,512]{1,0:T(8,128)}, f32[8,2,512]{2,1,0:T(2,128)}, bf16[512,512]{1,0:T(8,128)(2,1)}) custom-call(bf16[8,3,4,16,512]{4,3,2,1,0:T(8,128)(2,1)} %all_to_all.46.got_ref, bf16[512,512]{1,0:T(8,128)(2,1)} %q_ref.3, bf16[512,512]{1,0:T(8,128)(2,1)} %cot_ref.3, f32[1,512]{1,0:T(1,128)} %bitcast.26), custom_call_target="tpu_custom_call" | custom-call | tf_op jit(solution)/shard_map/pallas_call | solution.py:189
  92.2 9.9 %all_to_all.47.sums_ref = f32[8,2,512]{2,1,0:T(2,128)} all-to-all(f32[8,2,512]{2,1,0:T(2,128)} %get-tuple-element.16), channel_id=1, replica_groups=mesh['zh'=4,'zl'=2,'y'=4,'x'=4,'c'=2] {'x','c'}, dimensions={0} | all-to-all | bytes 65536 | tf_op jit(solution)/shard_map/all_to_all | solution.py:33
  102.1 6.3 %shard_map.122 = (bf16[8,3,4,16,512]{4,3,2,1,0:T(8,128)(2,1)}, f32[512,512]{1,0:T(8,128)}) custom-call(f32[8,2,512]{2,1,0:T(2,128)} %all_to_all.47.sums_ref, f32[512,512]{1,0:T(8,128)} %get-tuple-element.17.o_ref, f32[512,512]{1,0:T(8,128)} %get-tuple-element.18.p1_ref, f32[512,512]{1,0:T(8,128)} %get-tuple-element.19.p3_ref, bf16[512,512]{1,0:T(8,128)(2,1)} %q_ref.3, ...), custom_call_target="tpu_custom_call" | custom-call | tf_op jit(solution)/shard_map/pallas_call | solution.py:189
  108.4 25.1 %all_to_all.48 = bf16[8,3,4,16,512]{4,3,2,1,0:T(8,128)(2,1)S(1)} all-to-all(bf16[8,3,4,16,512]{4,3,2,1,0:T(8,128)(2,1)} %get-tuple-element.22), channel_id=1, replica_groups=mesh['zh'=4,'zl'=2,'y'=4,'x'=4,'c'=2] {'zl','y'}, dimensions={0} | all-to-all | bytes 3145728 | tf_op jit(solution)/shard_map/all_to_all | solution.py:33
  133.5 0.3 reduce_sum.122
  133.9 24.4 %all_to_all.49 = bf16[4,3,4,16,512]{4,3,2,1,0:T(8,128)(2,1)S(1)} all-to-all(bf16[4,3,4,16,512]{4,3,2,1,0:T(8,128)(2,1)S(1)} %broadcast_in_dim.43), channel_id=1, replica_groups=mesh['zh'=4,'zl'=2,'y'=4,'x'=4,'c'=2] {'zh'}, dimensions={0} | all-to-all | bytes 1572864 | tf_op jit(solution)/shard_map/all_to_all | solution.py:33
  158.5 0.9 fusion.20
  159.6 22.0 %all_to_all.50.got_ref = bf16[8,3,4,16,512]{4,3,2,1,0:T(8,128)(2,1)} all-to-all(bf16[8,3,4,16,512]{4,3,2,1,0:T(8,128)(2,1)S(1)} %broadcast_in_dim.47), channel_id=1, replica_groups=mesh['zh'=4,'zl'=2,'y'=4,'x'=4,'c'=2] {'zl','y'}, dimensions={0} | all-to-all | bytes 3145728 | tf_op jit(solution)/shard_map/all_to_all | solution.py:33
  181.6 7.4 %shard_map.123 = bf16[8,3,4,16,512]{4,3,2,1,0:T(8,128)(2,1)} custom-call(bf16[8,3,4,16,512]{4,3,2,1,0:T(8,128)(2,1)} %all_to_all.50.got_ref, bf16[512,512]{1,0:T(8,128)(2,1)} %k_ref.3, bf16[512,512]{1,0:T(8,128)(2,1)} %v_ref.3, f32[1,512]{1,0:T(1,128)} %r_ref.3, f32[512,512]{1,0:T(8,128)} %get-tuple-element.23.p1_ref, f32[512,512]{1,0:T(8,128)} %get-tuple-element.24.p3_ref, ...), custom_call_target="tpu_custom_call" | custom-call | tf_op jit(solution)/shard_map/pallas_call | solution.py:189
  189.0 6.1 %all-to-all-start.7 = ((bf16[8,3,4,16,512]{4,3,2,1,0:T(8,128)(2,1)}), bf16[8,3,4,16,512]{4,3,2,1,0:T(8,128)(2,1)S(1)}, u32[]{:S(2)}, u32[]{:S(2)}) async-start(bf16[8,3,4,16,512]{4,3,2,1,0:T(8,128)(2,1)} %shard_map.123), calls=%async_computation.7 | async-start | bytes 3145728 | tf_op jit(solution)/shard_map/all_to_all | solution.py:33
  195.0 0.7 slice.6
  195.8 3.4 %collective-permute-start = (bf16[256,512]{1,0:T(8,128)(2,1)}, bf16[256,512]{1,0:T(8,128)(2,1)}, u32[]{:S(2)}, u32[]{:S(2)}) collective-permute-start(bf16[256,512]{1,0:T(8,128)(2,1)} %slice.6), channel_id=1, source_target_pairs={{0,8},{8,16},{16,24},{24,32},{32,40},{40,48},{48,56},{56,64},{64,7... | collective-permute-start | bytes 786440 | tf_op jit(solution)/shard_map/ppermute | solution.py:255
  199.1 0.7 slice.7
  199.9 3.4 %collective-permute-start.1 = (bf16[256,512]{1,0:T(8,128)(2,1)}, bf16[256,512]{1,0:T(8,128)(2,1)}, u32[]{:S(2)}, u32[]{:S(2)}) collective-permute-start(bf16[256,512]{1,0:T(8,128)(2,1)} %slice.7), channel_id=1, source_target_pairs={{0,8},{8,16},{16,24},{24,32},{32,40},{40,48},{48,56},{56,64},{64,7... | collective-permute-start | bytes 786440 | tf_op jit(solution)/shard_map/ppermute | solution.py:255
  203.3 15.0 %collective-permute-done = bf16[256,512]{1,0:T(8,128)(2,1)} collective-permute-done((bf16[256,512]{1,0:T(8,128)(2,1)}, bf16[256,512]{1,0:T(8,128)(2,1)}, u32[]{:S(2)}, u32[]{:S(2)}) %collective-permute-start) | collective-permute-done | bytes 262176 | tf_op jit(solution)/shard_map/ppermute | solution.py:255
  218.3 1.8 fusion.21
  220.1 1.2 copy-done.3
  221.3 0.3 fusion.2
  221.6 0.3 reduce_sum.125
  221.9 0.7 copy.19
  222.6 9.5 %all-to-all-start.8 = ((bf16[4,3,16,512]{3,2,1,0:T(8,128)(2,1)}), bf16[4,3,16,512]{3,2,1,0:T(8,128)(2,1)S(1)}, u32[]{:S(2)}, u32[]{:S(2)}) async-start(bf16[4,3,16,512]{3,2,1,0:T(8,128)(2,1)} %copy.19), calls=%async_computation.8 | async-start | bytes 393216 | tf_op jit(solution)/shard_map/all_to_all | solution.py:33
  232.1 3.2 %fusion.3 = bf16[512,512]{1,0:T(8,128)(2,1)} fusion(f32[512,512]{1,0:T(8,128)} %get-tuple-element.21, bf16[512,512]{1,0:T(8,128)(2,1)S(1)} %copy-done.1, bf16[256,512]{1,0:T(8,128)(2,1)} %collective-permute-done.1, f32[512,768]{0,1:T(8,128)} %copy-done.3, f32[512]{0:T(512)S(1)} %fusion.2, f32[512]{0:T(512)S(1)} %get-tuple-element.36), kind=kOutput, calls=%fused_computation.10 | convolution fusion | flops 405929984 | bytes 3936256 | tf_op jit(solution)/shard_map/dot_general | solution.py:220
  235.3 5.5 %all-to-all-done.8 = bf16[4,3,16,512]{3,2,1,0:T(8,128)(2,1)S(1)} async-done(((bf16[4,3,16,512]{3,2,1,0:T(8,128)(2,1)}), bf16[4,3,16,512]{3,2,1,0:T(8,128)(2,1)S(1)}, u32[]{:S(2)}, u32[]{:S(2)}) %all-to-all-start.8) | async-done | bytes 196640 | tf_op jit(solution)/shard_map/all_to_all | solution.py:33
  240.8 1.8 bitcast_subtract_fusion
  (28 shorter events, 1.1 us)
Async XLA Ops:
  33.4 24.9 %all-to-all-start.1 = ((bf16[4,3,4,16,512]{4,3,2,1,0:T(8,128)(2,1)}), bf16[4,3,4,16,512]{4,3,2,1,0:T(8,128)(2,1)S(1)}, u32[]{:S(2)}, u32[]{:S(2)}) async-start(bf16[4,3,4,16,512]{4,3,2,1,0:T(8,128)(2,1)} %broadcast_in_dim.40), calls=%async_computation.1 | async-start | bytes 1572864 | tf_op jit(solution)/shard_map/all_to_all | solution.py:33
  189.0 6.1 %copy-start = (bf16[512,512]{1,0:T(8,128)(2,1)S(1)}, bf16[512,512]{1,0:T(8,128)(2,1)}, u32[]{:S(2)}) copy-start(bf16[512,512]{1,0:T(8,128)(2,1)} %k_ref.3) | copy-start | bytes 1572868
  189.0 10.2 %copy-start.1 = (bf16[512,512]{1,0:T(8,128)(2,1)S(1)}, bf16[512,512]{1,0:T(8,128)(2,1)}, u32[]{:S(2)}) copy-start(bf16[512,512]{1,0:T(8,128)(2,1)} %v_ref.3) | copy-start | bytes 1572868
  189.0 29.4 %copy-start.2 = (bf16[512,512]{1,0:T(8,128)(2,1)S(1)}, bf16[512,512]{1,0:T(8,128)(2,1)}, u32[]{:S(2)}) copy-start(bf16[512,512]{1,0:T(8,128)(2,1)} %q_ref.3) | copy-start | bytes 1572868
  189.0 32.6 %all-to-all-start.7 = ((bf16[8,3,4,16,512]{4,3,2,1,0:T(8,128)(2,1)}), bf16[8,3,4,16,512]{4,3,2,1,0:T(8,128)(2,1)S(1)}, u32[]{:S(2)}, u32[]{:S(2)}) async-start(bf16[8,3,4,16,512]{4,3,2,1,0:T(8,128)(2,1)} %shard_map.123), calls=%async_computation.7 | async-start | bytes 3145728 | tf_op jit(solution)/shard_map/all_to_all | solution.py:33
  195.8 22.6 %collective-permute-start = (bf16[256,512]{1,0:T(8,128)(2,1)}, bf16[256,512]{1,0:T(8,128)(2,1)}, u32[]{:S(2)}, u32[]{:S(2)}) collective-permute-start(bf16[256,512]{1,0:T(8,128)(2,1)} %slice.6), channel_id=1, source_target_pairs={{0,8},{8,16},{16,24},{24,32},{32,40},{40,48},{48,56},{56,64},{64,7... | collective-permute-start | bytes 786440 | tf_op jit(solution)/shard_map/ppermute | solution.py:255
  199.9 32.2 %collective-permute-start.1 = (bf16[256,512]{1,0:T(8,128)(2,1)}, bf16[256,512]{1,0:T(8,128)(2,1)}, u32[]{:S(2)}, u32[]{:S(2)}) collective-permute-start(bf16[256,512]{1,0:T(8,128)(2,1)} %slice.7), channel_id=1, source_target_pairs={{0,8},{8,16},{16,24},{24,32},{32,40},{40,48},{48,56},{56,64},{64,7... | collective-permute-start | bytes 786440 | tf_op jit(solution)/shard_map/ppermute | solution.py:255
  220.1 1.2 copy-start.3
  222.6 18.2 %all-to-all-start.8 = ((bf16[4,3,16,512]{3,2,1,0:T(8,128)(2,1)}), bf16[4,3,16,512]{3,2,1,0:T(8,128)(2,1)S(1)}, u32[]{:S(2)}, u32[]{:S(2)}) async-start(bf16[4,3,16,512]{3,2,1,0:T(8,128)(2,1)} %copy.19), calls=%async_computation.8 | async-start | bytes 393216 | tf_op jit(solution)/shard_map/all_to_all | solution.py:33
  232.0 8.8 %copy-start.4 = (f32[1,3,16,512]{3,2,1,0:T(8,128)S(1)}, f32[1,3,16,512]{3,2,1,0:T(8,128)}, u32[]{:S(2)}) copy-start(f32[1,3,16,512]{3,2,1,0:T(8,128)} %param.16) | copy-start | bytes 294916
  232.0 8.8 %copy-start.5 = (f32[1,3,16,512]{3,2,1,0:T(8,128)S(1)}, f32[1,3,16,512]{3,2,1,0:T(8,128)}, u32[]{:S(2)}) copy-start(f32[1,3,16,512]{3,2,1,0:T(8,128)} %param.17) | copy-start | bytes 294916

commit v2 on v1

--- a/solution.py
+++ b/solution.py
@@ -5,6 +5,7 @@
 from jax.experimental.pallas import tpu as pltpu
 from jax.sharding import Mesh
 from jax.sharding import PartitionSpec as P
+
 
 WIN = 256
 WIDTH = 4096
@@ -16,6 +17,7 @@
 NP = 8
 ROWS = 16
 BLOCK = 128
+VMEM_BYTES = 24 * 1024 * 1024
 beta_one = 0.9
 beta_two = 0.95
 adam_rate = 0.02
@@ -51,10 +53,6 @@
     return jnp.broadcast_to(row, (128, row.shape[1])).T
 
 
-def line(col):
-    return jnp.broadcast_to(col, (col.shape[0], 128)).T[:1, :]
-
-
 def blocks_of(count, body):
     def step(j, carry):
         body(pl.ds(pl.multiple_of(j * BLOCK, BLOCK), BLOCK))
@@ -66,13 +64,15 @@
 def put_grad(parts_ref, number, left, right):
     grad = mm(left[...], right[...], 0, 0).astype(bf16)
     for m in range(grad.shape[0] // ROWS):
-        parts_ref[m % NP, number, m // NP] = grad[m * ROWS : (m + 1) * ROWS]
+        at = (m // NP * 3 + number) * ROWS
+        parts_ref[m % NP, at : at + ROWS, :] = grad[m * ROWS : (m + 1) * ROWS]
 
 
 def take_matrices(parts_ref, out_ref):
     for number in range(out_ref.shape[0]):
         for m in range(out_ref.shape[1] // ROWS):
-            out_ref[number, m * ROWS : (m + 1) * ROWS, :] = parts_ref[m % NP, number, m // NP]
+            at = (m // NP * 3 + number) * ROWS
+            out_ref[number, m * ROWS : (m + 1) * ROWS, :] = parts_ref[m % NP, at : at + ROWS, :]
 
 
 def inner_kernel(k_ref, v_ref, r_ref, w_ref, parts_ref, p1_ref, p3_ref, b_ref, w_s, f_s, d1, d3, d2):
@@ -185,18 +185,33 @@
     put_grad(parts_ref, 2, v_ref, d2)
 
 
+def near(array):
+    return pltpu.with_memory_space_constraint(array, pltpu.VMEM)
+
+
 def called(kernel, outs, scratch, *args):
     return pl.pallas_call(
         kernel,
-        out_shape=[jax.ShapeDtypeStruct(*out) for out in outs],
+        out_shape=outs,
         in_specs=[pl.BlockSpec(memory_space=pltpu.VMEM)] * len(args),
         out_specs=[pl.BlockSpec(memory_space=pltpu.VMEM)] * len(outs),
         scratch_shapes=[pltpu.VMEM(*item) for item in scratch],
+        compiler_params=pltpu.CompilerParams(vmem_limit_bytes=VMEM_BYTES),
     )(*args)
 
 
-def to_owners(parts):
-    return totals(swapped(parts, PLANE)).astype(bf16)
+def reduce_rows(parts):
+    width = parts.shape[2]
+    some = swapped(parts, PLANE)
+    some = totals(some).astype(bf16)
+    got = swapped(some.reshape(NH, 3 * ROWS, width), "zh")
+    return totals(got).reshape(3, ROWS, width)
+
+
+def gather_rows(rows):
+    width = rows.shape[2]
+    some = swapped(copies(rows.reshape(3 * ROWS, width), NH), "zh")
+    return swapped(copies(some.reshape(-1, width), NP), PLANE)
 
 
 def attention_of(queries, keys, values, tail_k, tail_v, seq_index):
@@ -239,61 +254,56 @@
     )
 
 
-def local(queries, keys, values, rates, gain, cotangent, fast_init, first_moment, second_moment):
+def inner_local(queries, keys, values, rates, gain, cotangent, fast_init, first_moment, second_moment):
     tokens, dim = queries.shape
     zh = lax.axis_index("zh")
     plane = lax.axis_index(PLANE)
     weights = fast_init[0]
-    full, half = ((tokens, dim), f32), ((tokens, dim), bf16)
+    half = ((tokens, dim), bf16)
+    full, far = pltpu.VMEM((tokens, dim), f32), jax.ShapeDtypeStruct((tokens, dim), f32)
     side = ((tokens, 128), f32)
     mats = ((3, dim, dim), bf16)
-    owned = ((NP, 3, NH, ROWS, dim), bf16)
+    owned = pltpu.VMEM((NP, NH * 3 * ROWS, dim), bf16)
     gain_row = gain[None, :]
 
     last = NY * NP - 1
     pairs = [(i, i + 1) for i in range(last)]
-    tails = [lax.ppermute(a[tokens - WIN :], SEQ, pairs) for a in (keys, values)]
+    tails = jnp.stack([keys[tokens - WIN :], values[tokens - WIN :]])
+    tails = lax.ppermute(tails, SEQ, pairs)
 
     parts, first_pre, third_pre, back = called(
-        inner_kernel, [owned, full, full, full], [mats, side, half, half, half],
+        inner_kernel, [owned, far, far, far], [mats, side, half, half, half],
         keys, values, rates, weights,
     )
-    init_rows = lax.dynamic_index_in_dim(
-        weights.reshape(3, NH, NP, ROWS, dim), plane, 2, keepdims=False
-    )
-    moved_rows = init_rows - totals(swapped(copies(to_owners(parts), NH), "zh"))
-    rows = renorm(init_rows, moved_rows).astype(bf16)
-    renormed = swapped(copies(rows, NP), PLANE)
+    init_rows = lax.dynamic_slice_in_dim(weights, (zh * NP + plane) * ROWS, ROWS, 1)
+    moved_rows = init_rows - reduce_rows(parts)
+    renormed = gather_rows(renorm(init_rows, moved_rows).astype(bf16))
 
     fast_out, first_q, third_q, sums, second_w = called(
-        forward_kernel, [full, full, full, ((NP, 2, tokens), f32), half], [mats, side],
-        renormed, queries, cotangent, gain_row,
+        forward_kernel, [full, full, full, pltpu.VMEM((NP, 2, tokens), f32), pltpu.VMEM(*half)], [mats, side],
+        near(renormed), queries, cotangent, gain_row,
     )
     sums = swapped(sums, HEAD)
     parts, normed = called(
-        backward_kernel, [owned, full], [((2, tokens, 128), f32), half, half, half, half],
-        sums, fast_out, first_q, third_q, queries, cotangent, gain_row, second_w,
-    )
-    cot_rows = totals(swapped(copies(to_owners(parts), NH), "zh"))
+        backward_kernel, [owned, far], [((2, tokens, 128), f32), half, half, half, half],
+        near(sums), near(fast_out), near(first_q), near(third_q), queries, cotangent, gain_row,
+        near(second_w),
+    )
+    cot_rows = reduce_rows(parts)
     _, pull_norm = jax.vjp(renorm, init_rows, moved_rows)
     d_init_rows, d_moved_rows = pull_norm(cot_rows)
-    direction = swapped(copies(d_moved_rows.astype(bf16), NP), PLANE)
+    direction = gather_rows(d_moved_rows.astype(bf16))
 
     (parts,) = called(
         second_kernel, [owned], [mats, side, half, half, half],
-        direction, keys, values, rates, first_pre, third_pre, back,
-    )
-    second_terms = totals(swapped(jnp.moveaxis(to_owners(parts), 1, 0), "zh"))
-
-    def own(array):
-        return lax.dynamic_index_in_dim(array, zh, 1, keepdims=False)
-
-    grad_rows = own(d_init_rows + d_moved_rows) - second_terms
+        near(direction), keys, values, rates, first_pre, third_pre, back,
+    )
+    grad_rows = d_init_rows + d_moved_rows - reduce_rows(parts)
     attention = attention_of(
         queries, keys, values, tails[0], tails[1], zh * NP + plane
     )
     layer_out = (attention + normed).astype(bf16)
-    new = adam_step(own(init_rows), grad_rows, first_moment[0], second_moment[0])
+    new = adam_step(init_rows, grad_rows, first_moment[0], second_moment[0])
     return (layer_out, new[0][None], new[1][None], new[2][None])
 
 
@@ -311,7 +321,7 @@
         P(HEAD, None, SEQ, None),
     )
     return jax.shard_map(
-        local,
+        inner_local,
         mesh=split,
         in_specs=placed,
         out_specs=(

time: 243 us -> 227 us (0.934)
  Pallas kernels: 25.8 us -> 12.9 us
  starting transfers between devices: 29.8 us -> 23.7 us
  local copies, waits for them, and re-layouts: 4.74 us -> 9.39 us
    pallas_call x4, Pallas kernels: 25.8 us -> 12.9 us  [called(): pl.pallas_call(kernel, out_shape=outs, in_specs=[pl.BlockSpec(memory_spac...]
    all_to_all x3, waiting for transfers between devices: 22.8 us -> 15.1 us  [swapped(): return lax.all_to_all(parts, axes, split_axis=0, concat_axis=0, tiled=True)]
    unnamed x12 -> x38, local copies, waits for them, and re-layouts: 1.18 us -> 8.87 us
    ppermute x2 -> x1, waiting for transfers between devices: 15 us -> 20.4 us  [inner_local(): tails = lax.ppermute(tails, SEQ, pairs)]
    ppermute x2 -> x1, starting transfers between devices: 6.73 us -> 3.38 us  [inner_local(): tails = lax.ppermute(tails, SEQ, pairs)]
    all_to_all x3, starting transfers between devices: 23.1 us -> 20.3 us  [swapped(): return lax.all_to_all(parts, axes, split_axis=0, concat_axis=0, tiled=True)]
    reduce_sum x6, other arithmetic: 1.15 us -> 3.65 us  [totals(): return jnp.sum(parts.astype(f32), axis=0)]
    all_to_all x6 -> x8, blocking collectives: 133 us -> 134 us  [swapped(): return lax.all_to_all(parts, axes, split_axis=0, concat_axis=0, tiled=True)]
  transfers between devices with their start and end apart: 5 -> 4, of which waited for: 3 -> 3; matrix products, arithmetic and copies ran while one was open for 3% -> 2% of each run, Pallas kernels for 0% -> 0%
where the time goes in v2:
time: 227 us; the launch traced here: 226 us
  blocking collectives  134 us (59%)
  waiting for transfers between devices  35.5 us (16%)
  starting transfers between devices  23.7 us (10%)
  Pallas kernels  12.9 us (6%)
  local copies, waits for them, and re-layouts  9.39 us (4%)
  other arithmetic  6.16 us (3%)
  matrix products  3.74 us (2%)
    all_to_all x8, blocking collectives, swapped(): return lax.all_to_all(parts, axes, split_axis=0, concat_axis=0, tiled=True)  134 us
    ppermute x1, waiting for transfers between devices, inner_local(): tails = lax.ppermute(tails, SEQ, pairs)  20.4 us
    all_to_all x3, starting transfers between devices, swapped(): return lax.all_to_all(parts, axes, split_axis=0, concat_axis=0, tiled=True)  20.3 us
    all_to_all x3, waiting for transfers between devices, swapped(): return lax.all_to_all(parts, axes, split_axis=0, concat_axis=0, tiled=True)  15.1 us
    pallas_call x4, Pallas kernels, called(): pl.pallas_call(kernel, out_shape=outs, in_specs=[pl.BlockSpec(memory_spac...  12.9 us
    unnamed x38, local copies, waits for them, and re-layouts  8.87 us
  transfers between devices with their start and end apart: 4, of which 3 were waited for; matrix products, arithmetic and copies ran while one was open for 2% of the time, Pallas kernels for 0%

profile of v2, /device:TPU:24, one launch (start us, length us, event | category | flops | bytes accessed | tf_op | source)
XLA Modules:
  0.0 226.5 jit_solution(287922289478583734)
XLA Ops:
  0.6 1.9 copy-done
  2.5 1.0 copy-done.1
  3.6 1.0 copy-done.3
  5.3 2.9 %shard_map.120 = (bf16[8,192,512]{2,1,0:T(8,128)(2,1)S(1)}, f32[512,512]{1,0:T(8,128)S(1)}, f32[512,512]{1,0:T(8,128)S(1)}, f32[512,512]{1,0:T(8,128)S(1)}) custom-call(bf16[512,512]{1,0:T(8,128)(2,1)S(1)} %copy-done.1, bf16[512,512]{1,0:T(8,128)(2,1)S(1)} %copy-done.3, f32[1,512]{1,0:T(1,128)S(1)} %copy-done.12, f32[3,512,512]{2,1,0:T(8,128)S(1)} %bitcast.37), custom_call_target="tpu_custom_call" | custom-call | tf_op jit(solution)/shard_map/pallas_call | solution.py:193
  8.2 1.0 copy-done.7
  9.2 1.0 copy-done.9
  10.2 24.9 %all_to_all.55 = bf16[8,192,512]{2,1,0:T(8,128)(2,1)S(1)} all-to-all(bf16[8,192,512]{2,1,0:T(8,128)(2,1)S(1)} %get-tuple-element.15), channel_id=1, replica_groups=mesh['zh'=4,'zl'=2,'y'=4,'x'=4,'c'=2] {'zl','y'}, dimensions={0} | all-to-all | bytes 3145728 | tf_op jit(solution)/shard_map/all_to_all | solution.py:35
  35.1 0.9 reduce_sum.122
  36.0 7.6 %all-to-all-start.1 = ((bf16[4,48,512]{2,1,0:T(8,128)(2,1)}), bf16[4,48,512]{2,1,0:T(8,128)(2,1)S(1)}, u32[]{:S(2)}, u32[]{:S(2)}) async-start(bf16[4,48,512]{2,1,0:T(8,128)(2,1)} %bitcast.7), calls=%async_computation.1 | async-start | bytes 393216 | tf_op jit(solution)/shard_map/all_to_all | solution.py:35
  43.6 8.9 %all-to-all-done.1 = bf16[4,48,512]{2,1,0:T(8,128)(2,1)S(1)} async-done(((bf16[4,48,512]{2,1,0:T(8,128)(2,1)}), bf16[4,48,512]{2,1,0:T(8,128)(2,1)S(1)}, u32[]{:S(2)}, u32[]{:S(2)}) %all-to-all-start.1) | async-done | bytes 196640 | tf_op jit(solution)/shard_map/all_to_all | solution.py:35
  52.5 1.0 fusion.17
  53.7 11.7 %all_to_all.56 = bf16[4,48,512]{2,1,0:T(8,128)(2,1)S(1)} all-to-all(bf16[4,48,512]{2,1,0:T(8,128)(2,1)S(1)} %broadcast_in_dim.44), channel_id=1, replica_groups=mesh['zh'=4,'zl'=2,'y'=4,'x'=4,'c'=2] {'zh'}, dimensions={0} | all-to-all | bytes 393216 | tf_op jit(solution)/shard_map/all_to_all | solution.py:35
  65.6 20.1 %all_to_all.57.got_ref = bf16[8,192,512]{2,1,0:T(8,128)(2,1)S(1)} all-to-all(bf16[8,192,512]{2,1,0:T(8,128)(2,1)S(1)} %broadcast_in_dim.45), channel_id=1, replica_groups=mesh['zh'=4,'zl'=2,'y'=4,'x'=4,'c'=2] {'zl','y'}, dimensions={0} | all-to-all | bytes 3145728 | tf_op jit(solution)/shard_map/all_to_all | solution.py:35
  85.7 2.8 %shard_map.121 = (f32[512,512]{1,0:T(8,128)S(1)}, f32[512,512]{1,0:T(8,128)S(1)}, f32[512,512]{1,0:T(8,128)S(1)}, f32[8,2,512]{2,1,0:T(2,128)S(1)}, bf16[512,512]{1,0:T(8,128)(2,1)S(1)}) custom-call(bf16[8,192,512]{2,1,0:T(8,128)(2,1)S(1)} %all_to_all.57.got_ref, bf16[512,512]{1,0:T(8,128)(2,1)S(1)} %copy-done.6, bf16[512,512]{1,0:T(8,128)(2,1)S(1)} %copy-done.5, ...), custom_call_target="tpu_custom_call" | custom-call | tf_op jit(solution)/shard_map/pallas_call | solution.py:193
  88.5 9.5 %all_to_all.58.sums_ref = f32[8,2,512]{2,1,0:T(2,128)S(1)} all-to-all(f32[8,2,512]{2,1,0:T(2,128)S(1)} %get-tuple-element.16), channel_id=1, replica_groups=mesh['zh'=4,'zl'=2,'y'=4,'x'=4,'c'=2] {'x','c'}, dimensions={0} | all-to-all | bytes 65536 | tf_op jit(solution)/shard_map/all_to_all | solution.py:35
  98.0 2.7 %shard_map.122 = (bf16[8,192,512]{2,1,0:T(8,128)(2,1)S(1)}, f32[512,512]{1,0:T(8,128)S(1)}) custom-call(f32[8,2,512]{2,1,0:T(2,128)S(1)} %all_to_all.58.sums_ref, f32[512,512]{1,0:T(8,128)S(1)} %get-tuple-element.17.o_ref, f32[512,512]{1,0:T(8,128)S(1)} %get-tuple-element.18.p1_ref, f32[512,512]{1,0:T(8,128)S(1)} %get-tuple-element.19.p3_ref, ...), custom_call_target="tpu_custom_call" | custom-call | tf_op jit(solution)/shard_map/pallas_call | solution.py:193
  100.7 1.0 copy-done.14
  101.8 24.1 %all_to_all.59 = bf16[8,192,512]{2,1,0:T(8,128)(2,1)S(1)} all-to-all(bf16[8,192,512]{2,1,0:T(8,128)(2,1)S(1)} %get-tuple-element.22), channel_id=1, replica_groups=mesh['zh'=4,'zl'=2,'y'=4,'x'=4,'c'=2] {'zl','y'}, dimensions={0} | all-to-all | bytes 3145728 | tf_op jit(solution)/shard_map/all_to_all | solution.py:35
  126.2 11.9 %all_to_all.60 = bf16[4,48,512]{2,1,0:T(8,128)(2,1)S(1)} all-to-all(bf16[4,48,512]{2,1,0:T(8,128)(2,1)S(1)} %bitcast.46), channel_id=1, replica_groups=mesh['zh'=4,'zl'=2,'y'=4,'x'=4,'c'=2] {'zh'}, dimensions={0} | all-to-all | bytes 393216 | tf_op jit(solution)/shard_map/all_to_all | solution.py:35
  138.5 11.4 %all_to_all.61 = bf16[4,48,512]{2,1,0:T(8,128)(2,1)S(1)} all-to-all(bf16[4,48,512]{2,1,0:T(8,128)(2,1)S(1)} %broadcast_in_dim.52), channel_id=1, replica_groups=mesh['zh'=4,'zl'=2,'y'=4,'x'=4,'c'=2] {'zh'}, dimensions={0} | all-to-all | bytes 393216 | tf_op jit(solution)/shard_map/all_to_all | solution.py:35
  150.1 20.4 %all_to_all.62.got_ref = bf16[8,192,512]{2,1,0:T(8,128)(2,1)S(1)} all-to-all(bf16[8,192,512]{2,1,0:T(8,128)(2,1)S(1)} %broadcast_in_dim.53), channel_id=1, replica_groups=mesh['zh'=4,'zl'=2,'y'=4,'x'=4,'c'=2] {'zl','y'}, dimensions={0} | all-to-all | bytes 3145728 | tf_op jit(solution)/shard_map/all_to_all | solution.py:35
  170.6 4.5 %shard_map.123 = bf16[8,192,512]{2,1,0:T(8,128)(2,1)} custom-call(bf16[8,192,512]{2,1,0:T(8,128)(2,1)S(1)} %all_to_all.62.got_ref, bf16[512,512]{1,0:T(8,128)(2,1)S(1)} %copy-done.2, bf16[512,512]{1,0:T(8,128)(2,1)S(1)} %copy-done.4, f32[1,512]{1,0:T(1,128)S(1)} %copy-done.13, f32[512,512]{1,0:T(8,128)S(1)} %get-tuple-element.23.p1_ref, ...), custom_call_target="tpu_custom_call" | custom-call | tf_op jit(solution)/shard_map/pallas_call | solution.py:193
  175.0 6.6 %all-to-all-start.9 = ((bf16[8,192,512]{2,1,0:T(8,128)(2,1)}), bf16[8,192,512]{2,1,0:T(8,128)(2,1)}, u32[]{:S(2)}, u32[]{:S(2)}) async-start(bf16[8,192,512]{2,1,0:T(8,128)(2,1)} %shard_map.123), calls=%async_computation.9 | async-start | bytes 3145728 | tf_op jit(solution)/shard_map/all_to_all | solution.py:35
  181.7 3.4 %collective-permute-start = (bf16[2,256,512]{2,1,0:T(8,128)(2,1)S(1)}, bf16[2,256,512]{2,1,0:T(8,128)(2,1)S(1)}, u32[]{:S(2)}, u32[]{:S(2)}) collective-permute-start(bf16[2,256,512]{2,1,0:T(8,128)(2,1)S(1)} %pad_maximum_fusion), channel_id=1, source_target_pairs={{0,8},{8,16},{16,24},{24,32},{32,40},{40,48},{48,56},{56,64},{64,7... | collective-permute-start | bytes 1572872 | tf_op jit(solution)/shard_map/ppermute | solution.py:272
  185.1 20.4 %collective-permute-done = bf16[2,256,512]{2,1,0:T(8,128)(2,1)S(1)} collective-permute-done((bf16[2,256,512]{2,1,0:T(8,128)(2,1)S(1)}, bf16[2,256,512]{2,1,0:T(8,128)(2,1)S(1)}, u32[]{:S(2)}, u32[]{:S(2)}) %collective-permute-start) | collective-permute-done | bytes 524320 | tf_op jit(solution)/shard_map/ppermute | solution.py:272
  205.6 0.9 fusion.23
  206.4 1.2 copy-done.16
  207.9 2.4 %reduce_sum.132 = bf16[192,512]{1,0:T(8,128)(2,1)} reduce(bf16[8,192,512]{2,1,0:T(8,128)(2,1)} %all-to-all-done.9, bf16[]{:T(256)} %constant.62.clone.1), dimensions={0}, to_apply=%region_9.0 | reduce | flops 688128 | bytes 1769474 | tf_op jit(solution)/shard_map/reduce_sum | solution.py:43
  210.3 6.2 %all-to-all-start.10 = ((bf16[4,48,512]{2,1,0:T(8,128)(2,1)}), bf16[4,48,512]{2,1,0:T(8,128)(2,1)S(1)}, u32[]{:S(2)}, u32[]{:S(2)}) async-start(bf16[4,48,512]{2,1,0:T(8,128)(2,1)} %bitcast.16), calls=%async_computation.10 | async-start | bytes 393216 | tf_op jit(solution)/shard_map/all_to_all | solution.py:35
  216.4 2.9 %fusion.3 = bf16[512,512]{1,0:T(8,128)(2,1)} fusion(f32[512,512]{1,0:T(8,128)S(1)} %copy-done.15, bf16[512,512]{1,0:T(8,128)(2,1)S(1)} %copy-done.4, bf16[256,512]{1,0:T(8,128)(2,1)S(1)} %get-tuple-element.35, f32[512,768]{0,1:T(8,128)} %copy-done.16, f32[512]{0:T(512)S(1)} %fusion.2, f32[512]{0:T(512)S(1)} %get-tuple-element.38), kind=kOutput, calls=%fused_computation.8 | convolution fusion | flops 405929984 | bytes 3936256 | tf_op jit(solution)/shard_map/dot_general | solution.py:235
  219.3 6.3 %all-to-all-done.10 = bf16[4,48,512]{2,1,0:T(8,128)(2,1)S(1)} async-done(((bf16[4,48,512]{2,1,0:T(8,128)(2,1)}), bf16[4,48,512]{2,1,0:T(8,128)(2,1)S(1)}, u32[]{:S(2)}, u32[]{:S(2)}) %all-to-all-start.10) | async-done | bytes 196640 | tf_op jit(solution)/shard_map/all_to_all | solution.py:35
  225.6 0.9 divide_subtract_fusion
  (54 shorter events, 2.3 us)
Async XLA Ops:
  0.6 1.9 copy-start
  2.5 1.0 copy-start.1
  3.6 1.0 copy-start.3
  4.6 0.7 copy-start.12
  8.2 1.0 copy-start.7
  9.2 1.0 copy-start.9
  36.0 16.4 %all-to-all-start.1 = ((bf16[4,48,512]{2,1,0:T(8,128)(2,1)}), bf16[4,48,512]{2,1,0:T(8,128)(2,1)S(1)}, u32[]{:S(2)}, u32[]{:S(2)}) async-start(bf16[4,48,512]{2,1,0:T(8,128)(2,1)} %bitcast.7), calls=%async_computation.1 | async-start | bytes 393216 | tf_op jit(solution)/shard_map/all_to_all | solution.py:35
  65.6 20.1 %copy-start.5 = (bf16[512,512]{1,0:T(8,128)(2,1)S(1)}, bf16[512,512]{1,0:T(8,128)(2,1)}, u32[]{:S(2)}) copy-start(bf16[512,512]{1,0:T(8,128)(2,1)} %cot_ref.3) | copy-start | bytes 1572868
  65.6 20.1 %copy-start.6 = (bf16[512,512]{1,0:T(8,128)(2,1)S(1)}, bf16[512,512]{1,0:T(8,128)(2,1)}, u32[]{:S(2)}) copy-start(bf16[512,512]{1,0:T(8,128)(2,1)} %q_ref.3) | copy-start | bytes 1572868
  65.6 20.1 %copy-start.11 = (f32[512]{0:T(512)S(1)}, f32[512]{0:T(512)}, u32[]{:S(2)}) copy-start(f32[512]{0:T(512)} %param.13) | copy-start | bytes 6148
  100.7 1.0 copy-start.14
  150.0 20.5 %copy-start.2 = (bf16[512,512]{1,0:T(8,128)(2,1)S(1)}, bf16[512,512]{1,0:T(8,128)(2,1)}, u32[]{:S(2)}) copy-start(bf16[512,512]{1,0:T(8,128)(2,1)} %k_ref.3) | copy-start | bytes 1572868
  150.1 20.5 %copy-start.4 = (bf16[512,512]{1,0:T(8,128)(2,1)S(1)}, bf16[512,512]{1,0:T(8,128)(2,1)}, u32[]{:S(2)}) copy-start(bf16[512,512]{1,0:T(8,128)(2,1)} %v_ref.3) | copy-start | bytes 1572868
  150.1 20.5 %copy-start.8 = (f32[512,512]{1,0:T(8,128)S(1)}, f32[512,512]{1,0:T(8,128)}, u32[]{:S(2)}) copy-start(f32[512,512]{1,0:T(8,128)} %copy-done.7) | copy-start | bytes 3145732
  150.1 20.5 %copy-start.10 = (f32[512,512]{1,0:T(8,128)S(1)}, f32[512,512]{1,0:T(8,128)}, u32[]{:S(2)}) copy-start(f32[512,512]{1,0:T(8,128)} %copy-done.9) | copy-start | bytes 3145732
  150.1 20.5 %copy-start.13 = (f32[1,512]{1,0:T(1,128)S(1)}, f32[1,512]{1,0:T(1,128)}, u32[]{:S(2)}) copy-start(f32[1,512]{1,0:T(1,128)} %r_ref.3) | copy-start | bytes 6148
  175.0 32.8 %all-to-all-start.9 = ((bf16[8,192,512]{2,1,0:T(8,128)(2,1)}), bf16[8,192,512]{2,1,0:T(8,128)(2,1)}, u32[]{:S(2)}, u32[]{:S(2)}) async-start(bf16[8,192,512]{2,1,0:T(8,128)(2,1)} %shard_map.123), calls=%async_computation.9 | async-start | bytes 3145728 | tf_op jit(solution)/shard_map/all_to_all | solution.py:35
  181.7 23.8 %collective-permute-start = (bf16[2,256,512]{2,1,0:T(8,128)(2,1)S(1)}, bf16[2,256,512]{2,1,0:T(8,128)(2,1)S(1)}, u32[]{:S(2)}, u32[]{:S(2)}) collective-permute-start(bf16[2,256,512]{2,1,0:T(8,128)(2,1)S(1)} %pad_maximum_fusion), channel_id=1, source_target_pairs={{0,8},{8,16},{16,24},{24,32},{32,40},{40,48},{48,56},{56,64},{64,7... | collective-permute-start | bytes 1572872 | tf_op jit(solution)/shard_map/ppermute | solution.py:272
  206.4 1.2 copy-start.16
  207.6 8.8 %copy-start.15 = (f32[512,512]{1,0:T(8,128)S(1)}, f32[512,512]{1,0:T(8,128)}, u32[]{:S(2)}) copy-start(f32[512,512]{1,0:T(8,128)} %copy-done.14) | copy-start | bytes 3145732
  210.3 15.3 %all-to-all-start.10 = ((bf16[4,48,512]{2,1,0:T(8,128)(2,1)}), bf16[4,48,512]{2,1,0:T(8,128)(2,1)S(1)}, u32[]{:S(2)}, u32[]{:S(2)}) async-start(bf16[4,48,512]{2,1,0:T(8,128)(2,1)} %bitcast.16), calls=%async_computation.10 | async-start | bytes 393216 | tf_op jit(solution)/shard_map/all_to_all | solution.py:35
  216.4 9.2 %copy-start.17 = (f32[1,3,16,512]{3,2,1,0:T(8,128)S(1)}, f32[1,3,16,512]{3,2,1,0:T(8,128)}, u32[]{:S(2)}) copy-start(f32[1,3,16,512]{3,2,1,0:T(8,128)} %param.16) | copy-start | bytes 294916
  216.4 9.2 %copy-start.18 = (f32[1,3,16,512]{3,2,1,0:T(8,128)S(1)}, f32[1,3,16,512]{3,2,1,0:T(8,128)}, u32[]{:S(2)}) copy-start(f32[1,3,16,512]{3,2,1,0:T(8,128)} %param.17) | copy-start | bytes 294916

commit v3 on v2

--- a/solution.py
+++ b/solution.py
@@ -75,11 +75,16 @@
             out_ref[number, m * ROWS : (m + 1) * ROWS, :] = parts_ref[m % NP, at : at + ROWS, :]
 
 
-def inner_kernel(k_ref, v_ref, r_ref, w_ref, parts_ref, p1_ref, p3_ref, b_ref, w_s, f_s, d1, d3, d2):
+def inner_kernel(
+    seq_ref, k_ref, v_ref, r_ref, w_ref,
+    parts_ref, p1_ref, p3_ref, b_ref, own_ref, w_s, f_s, d1, d3, d2,
+):
     tokens, dim = k_ref.shape
     scale = dim ** (-0.5)
+    own = pl.ds(pl.multiple_of(seq_ref[0] * ROWS, ROWS), ROWS)
     for m in range(3):
         w_s[m] = w_ref[m].astype(bf16)
+        own_ref[m * ROWS : (m + 1) * ROWS, :] = w_ref[m, own, :]
     f_s[...] = columns(r_ref[...] * (-scale))
 
     def body(at):
@@ -126,11 +131,18 @@
 
 
 def backward_kernel(
-    sums_ref, o_ref, p1_ref, p3_ref, q_ref, cot_ref, gain_ref, w2_ref,
-    parts_ref, normed_ref, s_s, d1, d3, a_s, e_s,
+    seq_ref, sums_ref, o_ref, p1_ref, p3_ref, q_ref, cot_ref, gain_ref, w2_ref, k_ref, v_ref, tails_ref,
+    parts_ref, layer_ref, s_s, d1, d3, a_s, e_s, all_s,
 ):
     tokens, dim = q_ref.shape
     scale = dim ** (-0.5)
+    all_s[:, :WIN, :] = tails_ref[...]
+    all_s[0, WIN:, :] = k_ref[...]
+    all_s[1, WIN:, :] = v_ref[...]
+    span = BLOCK + WIN
+    ahead = lax.broadcasted_iota(jnp.int32, (BLOCK, span), 1)
+    behind = ahead - lax.broadcasted_iota(jnp.int32, (BLOCK, span), 0)
+    near_by = (behind > 0) & (behind <= WIN)
     sums = jnp.sum(sums_ref[...], axis=0)
     inverse = 1.0 / jnp.sqrt(sums[:1] / WIDTH + 1e-06)
     coef = sums[1:] * inverse * inverse * inverse / WIDTH
@@ -143,7 +155,14 @@
         weighted = cot_ref[at, :].astype(f32) * gain_ref[...]
         err = (scale * (weighted * inv - out * s_s[1, at, :][:, :1])).astype(bf16)
         e_s[at, :] = err
-        normed_ref[at, :] = out * inv * gain_ref[...]
+        window = pl.ds(at.start, span)
+        scores = scale * mm(q_ref[at, :], all_s[0, window, :], 1, 1)
+        known = near_by & (ahead + (seq_ref[0] * tokens + at.start) >= WIN)
+        scores = jnp.where(known, scores, -1e30)
+        expo = jnp.exp(scores - jnp.max(scores, axis=1, keepdims=True))
+        probs = expo / jnp.sum(expo, axis=1, keepdims=True)
+        attention = mm(probs, all_s[1, window, :], 1, 0)
+        layer_ref[at, :] = (attention + out * inv * gain_ref[...]).astype(bf16)
         back = mm(err, w2_ref[...], 1, 0)
         p3 = p3_ref[at, :]
         gate, gate1, _ = gates(p1_ref[at, :])
@@ -189,11 +208,43 @@
     return pltpu.with_memory_space_constraint(array, pltpu.VMEM)
 
 
+def total_kernel(got_ref, out_ref):
+    peers, height, _ = out_ref.shape
+    for m in range(peers):
+        out_ref[m] = totals(got_ref[:, m * height : (m + 1) * height, :]).astype(bf16)
+
+
+def means(array):
+    return jnp.mean(array, axis=1, keepdims=True)
+
+
+def moved_kernel(got_ref, own_ref, moved_ref, out_ref):
+    own = own_ref[...]
+    moved = own - totals(got_ref[...])
+    moved_ref[...] = moved
+    factor = jnp.sqrt(means(own * own)) / jnp.sqrt(means(moved * moved) + 1e-06)
+    out_ref[...] = copies((moved * factor).astype(bf16), NH)
+
+
+def pulled_kernel(got_ref, own_ref, moved_ref, part_ref, out_ref):
+    own, moved = own_ref[...], moved_ref[...]
+    cot = totals(got_ref[...])
+    target = jnp.sqrt(means(own * own))
+    inverse = 1.0 / jnp.sqrt(means(moved * moved) + 1e-06)
+    along = means(cot * moved) * inverse
+    d_moved = (target * inverse) * (cot - moved * (along * inverse))
+    part_ref[...] = d_moved + own * (along / target)
+    out_ref[...] = copies(d_moved.astype(bf16), NH)
+
+
 def called(kernel, outs, scratch, *args):
     return pl.pallas_call(
         kernel,
         out_shape=outs,
-        in_specs=[pl.BlockSpec(memory_space=pltpu.VMEM)] * len(args),
+        in_specs=[
+            pl.BlockSpec(memory_space=pltpu.SMEM if arg.dtype == jnp.int32 else pltpu.VMEM)
+            for arg in args
+        ],
         out_specs=[pl.BlockSpec(memory_space=pltpu.VMEM)] * len(outs),
         scratch_shapes=[pltpu.VMEM(*item) for item in scratch],
         compiler_params=pltpu.CompilerParams(vmem_limit_bytes=VMEM_BYTES),
@@ -201,45 +252,15 @@
 
 
 def reduce_rows(parts):
-    width = parts.shape[2]
     some = swapped(parts, PLANE)
-    some = totals(some).astype(bf16)
-    got = swapped(some.reshape(NH, 3 * ROWS, width), "zh")
-    return totals(got).reshape(3, ROWS, width)
+    shape = (NH, parts.shape[1] // NH, parts.shape[2])
+    (some,) = called(total_kernel, [pltpu.VMEM(shape, bf16)], [], near(some))
+    return swapped(some, "zh")
 
 
 def gather_rows(rows):
-    width = rows.shape[2]
-    some = swapped(copies(rows.reshape(3 * ROWS, width), NH), "zh")
-    return swapped(copies(some.reshape(-1, width), NP), PLANE)
-
-
-def attention_of(queries, keys, values, tail_k, tail_v, seq_index):
-    tok_rows, head_dim = queries.shape
-    key_all = jnp.concatenate([tail_k, keys], axis=0)
-    value_all = jnp.concatenate([tail_v, values], axis=0)
-    scores = lax.dot_general(
-        queries, key_all, (((1,), (1,)), ((), ())), preferred_element_type=f32
-    ) * head_dim ** (-0.5)
-    query_pos = jnp.arange(tok_rows, dtype=jnp.int32)[:, None]
-    key_pos = jnp.arange(tok_rows + WIN, dtype=jnp.int32)[None, :] - WIN
-    in_window = (
-        (key_pos <= query_pos)
-        & (key_pos > query_pos - WIN)
-        & (key_pos + seq_index * tok_rows >= 0)
-    )
-    scores = jnp.where(in_window, scores, -1e30)
-    row_max = jnp.max(scores, axis=-1, keepdims=True)
-    expo = jnp.exp(scores - row_max)
-    probs = (expo / jnp.sum(expo, axis=-1, keepdims=True)).astype(bf16)
-    return jnp.dot(probs, value_all, preferred_element_type=f32)
-
-
-def renorm(weights, updated):
-    target = jnp.sqrt(jnp.mean(weights * weights, axis=-1, keepdims=True))
-    return updated * (
-        target / jnp.sqrt(jnp.mean(updated * updated, axis=-1, keepdims=True) + 1e-06)
-    )
+    some = swapped(rows, "zh")
+    return swapped(copies(some.reshape(-1, rows.shape[2]), NP), PLANE)
 
 
 def adam_step(weights, gradient, first_moment, second_moment):
@@ -256,14 +277,15 @@
 
 def inner_local(queries, keys, values, rates, gain, cotangent, fast_init, first_moment, second_moment):
     tokens, dim = queries.shape
-    zh = lax.axis_index("zh")
-    plane = lax.axis_index(PLANE)
-    weights = fast_init[0]
+    seq = lax.axis_index(SEQ).astype(jnp.int32).reshape(1)
     half = ((tokens, dim), bf16)
-    full, far = pltpu.VMEM((tokens, dim), f32), jax.ShapeDtypeStruct((tokens, dim), f32)
+    full = pltpu.VMEM((tokens, dim), f32)
+    far = jax.ShapeDtypeStruct((tokens, dim), f32)
     side = ((tokens, 128), f32)
     mats = ((3, dim, dim), bf16)
     owned = pltpu.VMEM((NP, NH * 3 * ROWS, dim), bf16)
+    rows = pltpu.VMEM((3 * ROWS, dim), f32)
+    alike = pltpu.VMEM((NH, 3 * ROWS, dim), bf16)
     gain_row = gain[None, :]
 
     last = NY * NP - 1
@@ -271,39 +293,37 @@
     tails = jnp.stack([keys[tokens - WIN :], values[tokens - WIN :]])
     tails = lax.ppermute(tails, SEQ, pairs)
 
-    parts, first_pre, third_pre, back = called(
-        inner_kernel, [owned, far, far, far], [mats, side, half, half, half],
-        keys, values, rates, weights,
-    )
-    init_rows = lax.dynamic_slice_in_dim(weights, (zh * NP + plane) * ROWS, ROWS, 1)
-    moved_rows = init_rows - reduce_rows(parts)
-    renormed = gather_rows(renorm(init_rows, moved_rows).astype(bf16))
+    parts, first_pre, third_pre, back, own = called(
+        inner_kernel, [owned, far, far, far, rows], [mats, side, half, half, half],
+        seq, keys, values, rates, fast_init[0],
+    )
+    got = reduce_rows(parts)
+    moved, out = called(moved_kernel, [rows, alike], [], near(got), near(own))
+    renormed = gather_rows(out)
 
     fast_out, first_q, third_q, sums, second_w = called(
-        forward_kernel, [full, full, full, pltpu.VMEM((NP, 2, tokens), f32), pltpu.VMEM(*half)], [mats, side],
+        forward_kernel,
+        [full, full, full, pltpu.VMEM((NP, 2, tokens), f32), pltpu.VMEM(*half)], [mats, side],
         near(renormed), queries, cotangent, gain_row,
     )
     sums = swapped(sums, HEAD)
-    parts, normed = called(
-        backward_kernel, [owned, far], [((2, tokens, 128), f32), half, half, half, half],
-        near(sums), near(fast_out), near(first_q), near(third_q), queries, cotangent, gain_row,
-        near(second_w),
-    )
-    cot_rows = reduce_rows(parts)
-    _, pull_norm = jax.vjp(renorm, init_rows, moved_rows)
-    d_init_rows, d_moved_rows = pull_norm(cot_rows)
-    direction = gather_rows(d_moved_rows.astype(bf16))
+    parts, layer_out = called(
+        backward_kernel, [owned, jax.ShapeDtypeStruct(*half)],
+        [((2, tokens, 128), f32), half, half, half, half, ((2, tokens + WIN, dim), bf16)],
+        seq, near(sums), near(fast_out), near(first_q), near(third_q), queries, cotangent, gain_row,
+        near(second_w), keys, values, tails,
+    )
+    got = reduce_rows(parts)
+    part, out = called(pulled_kernel, [rows, alike], [], near(got), near(own), near(moved))
+    direction = gather_rows(out)
 
     (parts,) = called(
         second_kernel, [owned], [mats, side, half, half, half],
         near(direction), keys, values, rates, first_pre, third_pre, back,
     )
-    grad_rows = d_init_rows + d_moved_rows - reduce_rows(parts)
-    attention = attention_of(
-        queries, keys, values, tails[0], tails[1], zh * NP + plane
-    )
-    layer_out = (attention + normed).astype(bf16)
-    new = adam_step(init_rows, grad_rows, first_moment[0], second_moment[0])
+    grad_rows = part - totals(reduce_rows(parts))
+    shape = first_moment[0].shape
+    new = adam_step(own.reshape(shape), grad_rows.reshape(shape), first_moment[0], second_moment[0])
     return (layer_out, new[0][None], new[1][None], new[2][None])
 
 

time: 227 us -> 230 us (1.013)
  blocking collectives: 134 us -> 159 us
  waiting for transfers between devices: 35.5 us -> 19.5 us
  starting transfers between devices: 23.7 us -> 13.4 us
  local copies, waits for them, and re-layouts: 9.39 us -> 16.8 us
  other arithmetic: 6.16 us -> 1.65 us
  matrix products: 3.74 us -> 0 us
  Pallas kernels: 12.9 us -> 16 us
    all_to_all x8 -> x9, blocking collectives: 134 us -> 159 us  [swapped(): return lax.all_to_all(parts, axes, split_axis=0, concat_axis=0, tiled=True)]
    ppermute x1, waiting for transfers between devices: 20.4 us -> 0.01 us  [inner_local(): tails = lax.ppermute(tails, SEQ, pairs)]
    all_to_all x3 -> x2, starting transfers between devices: 20.3 us -> 10.1 us  [swapped(): return lax.all_to_all(parts, axes, split_axis=0, concat_axis=0, tiled=True)]
    unnamed x38 -> x54, local copies, waits for them, and re-layouts: 8.87 us -> 15.3 us
    all_to_all x3 -> x2, waiting for transfers between devices: 15.1 us -> 19.5 us  [swapped(): return lax.all_to_all(parts, axes, split_axis=0, concat_axis=0, tiled=True)]
    dot_general x2 -> x0, matrix products: 3.74 us -> none  [the longest x1 2.88 us: attention_of(): return jnp.dot(probs, value_all, preferred_element_type=f32)]
    reduce_sum x6 -> x1, other arithmetic: 3.65 us -> 0.03 us  [totals(): return jnp.sum(parts.astype(f32), axis=0)]
    pallas_call x4 -> x9, Pallas kernels: 12.9 us -> 16 us  [called(): pl.pallas_call(kernel, out_shape=outs, in_specs=[pl.BlockSpec(memory_spac...]
  transfers between devices with their start and end apart: 4 -> 3, of which waited for: 3 -> 2; matrix products, arithmetic and copies ran while one was open for 2% -> 0% of each run, Pallas kernels for 0% -> 1%
where the time goes in v3:
time: 230 us; the launch traced here: 227 us
  blocking collectives  159 us (69%)
  waiting for transfers between devices  19.5 us (8%)
  local copies, waits for them, and re-layouts  16.8 us (7%)
  Pallas kernels  16 us (7%)
  starting transfers between devices  13.4 us (6%)
    all_to_all x9, blocking collectives, swapped(): return lax.all_to_all(parts, axes, split_axis=0, concat_axis=0, tiled=True)  159 us
    all_to_all x2, waiting for transfers between devices, swapped(): return lax.all_to_all(parts, axes, split_axis=0, concat_axis=0, tiled=True)  19.5 us
    pallas_call x9, Pallas kernels, called(): pl.pallas_call(kernel, out_shape=outs, in_specs=[pl.BlockSpec(memory_spac...  16 us
    unnamed x54, local copies, waits for them, and re-layouts  15.3 us
    all_to_all x2, starting transfers between devices, swapped(): return lax.all_to_all(parts, axes, split_axis=0, concat_axis=0, tiled=True)  10.1 us
  transfers between devices with their start and end apart: 3, of which 2 were waited for; matrix products, arithmetic and copies ran while one was open for 0% of the time, Pallas kernels for 1%

profile of v3, /device:TPU:24, one launch (start us, length us, event | category | flops | bytes accessed | tf_op | source)
XLA Modules:
  0.0 227.5 jit_solution(4392494591250258827)
XLA Ops:
  0.7 1.0 copy-done
  1.7 1.0 copy-done.2
  2.7 1.9 copy-done.4
  5.3 2.9 %shard_map.120 = (bf16[8,192,512]{2,1,0:T(8,128)(2,1)S(1)}, f32[512,512]{1,0:T(8,128)S(1)}, f32[512,512]{1,0:T(8,128)S(1)}, f32[512,512]{1,0:T(8,128)S(1)}, f32[48,512]{1,0:T(8,128)S(1)}) custom-call(s32[1]{0:T(128)} %bitcast.seq_ref, bf16[512,512]{1,0:T(8,128)(2,1)S(1)} %copy-done, bf16[512,512]{1,0:T(8,128)(2,1)S(1)} %copy-done.2, ...), custom_call_target="tpu_custom_call" | custom-call | tf_op jit(solution)/shard_map/pallas_call | solution.py:241
  8.3 24.9 %all_to_all.55.got_ref = bf16[8,192,512]{2,1,0:T(8,128)(2,1)S(1)} all-to-all(bf16[8,192,512]{2,1,0:T(8,128)(2,1)S(1)} %get-tuple-element.20), channel_id=1, replica_groups=mesh['zh'=4,'zl'=2,'y'=4,'x'=4,'c'=2] {'zl','y'}, dimensions={0} | all-to-all | bytes 3145728 | tf_op jit(solution)/shard_map/all_to_all | solution.py:35
  33.4 16.8 %all_to_all.56.got_ref = bf16[4,48,512]{2,1,0:T(8,128)(2,1)S(1)} all-to-all(bf16[4,48,512]{2,1,0:T(8,128)(2,1)S(1)} %shard_map.121), channel_id=1, replica_groups=mesh['zh'=4,'zl'=2,'y'=4,'x'=4,'c'=2] {'zh'}, dimensions={0} | all-to-all | bytes 393216 | tf_op jit(solution)/shard_map/all_to_all | solution.py:35
  50.4 11.4 %all_to_all.57 = bf16[4,48,512]{2,1,0:T(8,128)(2,1)S(1)} all-to-all(bf16[4,48,512]{2,1,0:T(8,128)(2,1)S(1)} %get-tuple-element.22), channel_id=1, replica_groups=mesh['zh'=4,'zl'=2,'y'=4,'x'=4,'c'=2] {'zh'}, dimensions={0} | all-to-all | bytes 393216 | tf_op jit(solution)/shard_map/all_to_all | solution.py:35
  61.8 1.3 broadcast_in_dim.12
  63.1 5.8 %all-to-all-start.3 = ((bf16[8,192,512]{2,1,0:T(8,128)(2,1)}), bf16[8,192,512]{2,1,0:T(8,128)(2,1)S(1)}, u32[]{:S(2)}, u32[]{:S(2)}) async-start(bf16[8,192,512]{2,1,0:T(8,128)(2,1)} %broadcast_in_dim.12), calls=%async_computation.3 | async-start | bytes 3145728 | tf_op jit(solution)/shard_map/all_to_all | solution.py:35
  69.0 0.9 pad_maximum_fusion
  69.8 3.4 %collective-permute-start = (bf16[2,256,512]{2,1,0:T(8,128)(2,1)}, bf16[2,256,512]{2,1,0:T(8,128)(2,1)}, u32[]{:S(2)}, u32[]{:S(2)}) collective-permute-start(bf16[2,256,512]{2,1,0:T(8,128)(2,1)} %pad_maximum_fusion), channel_id=1, source_target_pairs={{0,8},{8,16},{16,24},{24,32},{32,40},{40,48},{48,56},{56,64},{64,7... | collective-permute-start | bytes 1572872 | tf_op jit(solution)/shard_map/ppermute | solution.py:294
  73.2 14.1 %all-to-all-done.3.got_ref = bf16[8,192,512]{2,1,0:T(8,128)(2,1)S(1)} async-done(((bf16[8,192,512]{2,1,0:T(8,128)(2,1)}), bf16[8,192,512]{2,1,0:T(8,128)(2,1)S(1)}, u32[]{:S(2)}, u32[]{:S(2)}) %all-to-all-start.3) | async-done | bytes 1572896 | tf_op jit(solution)/shard_map/all_to_all | solution.py:35
  87.3 1.0 copy-done.6
  88.4 3.4 %shard_map.123 = (f32[512,512]{1,0:T(8,128)S(1)}, f32[512,512]{1,0:T(8,128)S(1)}, f32[512,512]{1,0:T(8,128)S(1)}, f32[8,2,512]{2,1,0:T(2,128)}, bf16[512,512]{1,0:T(8,128)(2,1)S(1)}) custom-call(bf16[8,192,512]{2,1,0:T(8,128)(2,1)S(1)} %all-to-all-done.3.got_ref, bf16[512,512]{1,0:T(8,128)(2,1)S(1)} %copy-done.5, bf16[512,512]{1,0:T(8,128)(2,1)S(1)} %copy-done.6, ...), custom_call_target="tpu_custom_call" | custom-call | tf_op jit(solution)/shard_map/pallas_call | solution.py:241
  91.7 1.0 copy-done.14
  92.8 1.0 copy-done.16
  93.8 1.0 copy-done.18
  95.5 4.3 %all-to-all-start.4 = ((f32[8,2,512]{2,1,0:T(2,128)}), f32[8,2,512]{2,1,0:T(2,128)S(1)}, u32[]{:S(2)}, u32[]{:S(2)}) async-start(f32[8,2,512]{2,1,0:T(2,128)} %get-tuple-element.23), calls=%async_computation.4 | async-start | bytes 65536 | tf_op jit(solution)/shard_map/all_to_all | solution.py:35
  99.8 5.4 %all-to-all-done.4.sums_ref = f32[8,2,512]{2,1,0:T(2,128)S(1)} async-done(((f32[8,2,512]{2,1,0:T(2,128)}), f32[8,2,512]{2,1,0:T(2,128)S(1)}, u32[]{:S(2)}, u32[]{:S(2)}) %all-to-all-start.4) | async-done | bytes 32800 | tf_op jit(solution)/shard_map/all_to_all | solution.py:35
  105.3 1.0 copy-done.7
  106.3 1.2 copy-done.15
  107.5 1.2 copy-done.17
  108.8 1.2 copy-done.19
  110.0 1.0 copy-done.21
  111.0 5.5 %shard_map.124 = (bf16[8,192,512]{2,1,0:T(8,128)(2,1)S(1)}, bf16[512,512]{1,0:T(8,128)(2,1)}) custom-call(s32[1]{0:T(128)} %bitcast.seq_ref, f32[8,2,512]{2,1,0:T(2,128)S(1)} %all-to-all-done.4.sums_ref, f32[512,512]{1,0:T(8,128)S(1)} %copy-done.15, f32[512,512]{1,0:T(8,128)S(1)} %copy-done.17, f32[512,512]{1,0:T(8,128)S(1)} %copy-done.19, ...), custom_call_target="tpu_custom_call" | custom-call | tf_op jit(solution)/shard_map/pallas_call | solution.py:241
  116.6 25.1 %all_to_all.58.got_ref = bf16[8,192,512]{2,1,0:T(8,128)(2,1)S(1)} all-to-all(bf16[8,192,512]{2,1,0:T(8,128)(2,1)S(1)} %get-tuple-element.29), channel_id=1, replica_groups=mesh['zh'=4,'zl'=2,'y'=4,'x'=4,'c'=2] {'zl','y'}, dimensions={0} | all-to-all | bytes 3145728 | tf_op jit(solution)/shard_map/all_to_all | solution.py:35
  141.9 17.3 %all_to_all.59.got_ref = bf16[4,48,512]{2,1,0:T(8,128)(2,1)S(1)} all-to-all(bf16[4,48,512]{2,1,0:T(8,128)(2,1)S(1)} %shard_map.125), channel_id=1, replica_groups=mesh['zh'=4,'zl'=2,'y'=4,'x'=4,'c'=2] {'zh'}, dimensions={0} | all-to-all | bytes 393216 | tf_op jit(solution)/shard_map/all_to_all | solution.py:35
  159.4 11.5 %all_to_all.60 = bf16[4,48,512]{2,1,0:T(8,128)(2,1)S(1)} all-to-all(bf16[4,48,512]{2,1,0:T(8,128)(2,1)S(1)} %get-tuple-element.32), channel_id=1, replica_groups=mesh['zh'=4,'zl'=2,'y'=4,'x'=4,'c'=2] {'zh'}, dimensions={0} | all-to-all | bytes 393216 | tf_op jit(solution)/shard_map/all_to_all | solution.py:35
  171.0 20.2 %all_to_all.61.got_ref = bf16[8,192,512]{2,1,0:T(8,128)(2,1)S(1)} all-to-all(bf16[8,192,512]{2,1,0:T(8,128)(2,1)S(1)} %broadcast_in_dim.14), channel_id=1, replica_groups=mesh['zh'=4,'zl'=2,'y'=4,'x'=4,'c'=2] {'zl','y'}, dimensions={0} | all-to-all | bytes 3145728 | tf_op jit(solution)/shard_map/all_to_all | solution.py:35
  191.2 3.3 %shard_map.127 = bf16[8,192,512]{2,1,0:T(8,128)(2,1)S(1)} custom-call(bf16[8,192,512]{2,1,0:T(8,128)(2,1)S(1)} %all_to_all.61.got_ref, bf16[512,512]{1,0:T(8,128)(2,1)S(1)} %copy-done.1, bf16[512,512]{1,0:T(8,128)(2,1)S(1)} %copy-done.3, f32[1,512]{1,0:T(1,128)S(1)} %copy-done.24, f32[512,512]{1,0:T(8,128)S(1)} %copy-done.9, f32[512,512]{1,0:T(8,128)S(1)} %copy-done.11, ...), custom_call_target="tpu_custom_call" | custom-call | tf_op jit(solution)/shard_map/pallas_call | solution.py:241
  194.6 18.4 %all_to_all.62.got_ref = bf16[8,192,512]{2,1,0:T(8,128)(2,1)S(1)} all-to-all(bf16[8,192,512]{2,1,0:T(8,128)(2,1)S(1)} %shard_map.127), channel_id=1, replica_groups=mesh['zh'=4,'zl'=2,'y'=4,'x'=4,'c'=2] {'zl','y'}, dimensions={0} | all-to-all | bytes 3145728 | tf_op jit(solution)/shard_map/all_to_all | solution.py:35
  213.1 13.5 %all_to_all.63 = bf16[4,48,512]{2,1,0:T(8,128)(2,1)S(1)} all-to-all(bf16[4,48,512]{2,1,0:T(8,128)(2,1)S(1)} %shard_map.128), channel_id=1, replica_groups=mesh['zh'=4,'zl'=2,'y'=4,'x'=4,'c'=2] {'zh'}, dimensions={0} | all-to-all | bytes 393216 | tf_op jit(solution)/shard_map/all_to_all | solution.py:35
  (53 shorter events, 3.4 us)
Async XLA Ops:
  0.6 1.0 copy-start
  1.7 1.0 copy-start.2
  2.7 1.9 copy-start.4
  4.6 0.7 copy-start.23
  8.2 24.9 %copy-start.8 = (f32[512,512]{1,0:T(8,128)}, f32[512,512]{1,0:T(8,128)S(1)}, u32[]{:S(2)}) copy-start(f32[512,512]{1,0:T(8,128)S(1)} %get-tuple-element.33.p1_ref) | copy-start | bytes 3145732
  8.3 24.9 %copy-start.10 = (f32[512,512]{1,0:T(8,128)}, f32[512,512]{1,0:T(8,128)S(1)}, u32[]{:S(2)}) copy-start(f32[512,512]{1,0:T(8,128)S(1)} %get-tuple-element.34.p3_ref) | copy-start | bytes 3145732
  8.3 24.9 %copy-start.12 = (f32[512,512]{1,0:T(8,128)}, f32[512,512]{1,0:T(8,128)S(1)}, u32[]{:S(2)}) copy-start(f32[512,512]{1,0:T(8,128)S(1)} %get-tuple-element.35.b_ref) | copy-start | bytes 3145732
  63.1 5.8 %copy-start.1 = (bf16[512,512]{1,0:T(8,128)(2,1)S(1)}, bf16[512,512]{1,0:T(8,128)(2,1)}, u32[]{:S(2)}) copy-start(bf16[512,512]{1,0:T(8,128)(2,1)} %k_ref.5) | copy-start | bytes 1572868
  63.1 5.8 %copy-start.3 = (bf16[512,512]{1,0:T(8,128)(2,1)S(1)}, bf16[512,512]{1,0:T(8,128)(2,1)}, u32[]{:S(2)}) copy-start(bf16[512,512]{1,0:T(8,128)(2,1)} %v_ref.5) | copy-start | bytes 1572868
  63.1 24.2 %all-to-all-start.3 = ((bf16[8,192,512]{2,1,0:T(8,128)(2,1)}), bf16[8,192,512]{2,1,0:T(8,128)(2,1)S(1)}, u32[]{:S(2)}, u32[]{:S(2)}) async-start(bf16[8,192,512]{2,1,0:T(8,128)(2,1)} %broadcast_in_dim.12), calls=%async_computation.3 | async-start | bytes 3145728 | tf_op jit(solution)/shard_map/all_to_all | solution.py:35
  68.9 18.4 %copy-start.5 = (bf16[512,512]{1,0:T(8,128)(2,1)S(1)}, bf16[512,512]{1,0:T(8,128)(2,1)}, u32[]{:S(2)}) copy-start(bf16[512,512]{1,0:T(8,128)(2,1)} %q_ref.3) | copy-start | bytes 1572868
  68.9 18.4 %copy-start.22 = (f32[512]{0:T(512)S(1)}, f32[512]{0:T(512)}, u32[]{:S(2)}) copy-start(f32[512]{0:T(512)} %param.13) | copy-start | bytes 6148
  69.8 30.0 %collective-permute-start = (bf16[2,256,512]{2,1,0:T(8,128)(2,1)}, bf16[2,256,512]{2,1,0:T(8,128)(2,1)}, u32[]{:S(2)}, u32[]{:S(2)}) collective-permute-start(bf16[2,256,512]{2,1,0:T(8,128)(2,1)} %pad_maximum_fusion), channel_id=1, source_target_pairs={{0,8},{8,16},{16,24},{24,32},{32,40},{40,48},{48,56},{56,64},{64,7... | collective-permute-start | bytes 1572872 | tf_op jit(solution)/shard_map/ppermute | solution.py:294
  87.3 1.0 copy-start.6
  91.7 1.0 copy-start.14
  92.8 1.0 copy-start.16
  93.8 1.0 copy-start.18
  94.7 0.8 copy-start.20
  95.5 9.7 %all-to-all-start.4 = ((f32[8,2,512]{2,1,0:T(2,128)}), f32[8,2,512]{2,1,0:T(2,128)S(1)}, u32[]{:S(2)}, u32[]{:S(2)}) async-start(f32[8,2,512]{2,1,0:T(2,128)} %get-tuple-element.23), calls=%async_computation.4 | async-start | bytes 65536 | tf_op jit(solution)/shard_map/all_to_all | solution.py:35
  105.3 1.0 copy-start.7
  106.3 1.2 copy-start.15
  107.5 1.2 copy-start.17
  108.7 1.2 copy-start.19
  110.0 1.0 copy-start.21
  171.0 20.2 %copy-start.9 = (f32[512,512]{1,0:T(8,128)S(1)}, f32[512,512]{1,0:T(8,128)}, u32[]{:S(2)}) copy-start(f32[512,512]{1,0:T(8,128)} %copy-done.8) | copy-start | bytes 3145732
  171.0 20.2 %copy-start.11 = (f32[512,512]{1,0:T(8,128)S(1)}, f32[512,512]{1,0:T(8,128)}, u32[]{:S(2)}) copy-start(f32[512,512]{1,0:T(8,128)} %copy-done.10) | copy-start | bytes 3145732
  171.0 20.2 %copy-start.13 = (f32[512,512]{1,0:T(8,128)S(1)}, f32[512,512]{1,0:T(8,128)}, u32[]{:S(2)}) copy-start(f32[512,512]{1,0:T(8,128)} %copy-done.12) | copy-start | bytes 3145732
  171.0 20.2 %copy-start.24 = (f32[1,512]{1,0:T(1,128)S(1)}, f32[1,512]{1,0:T(1,128)}, u32[]{:S(2)}) copy-start(f32[1,512]{1,0:T(1,128)} %r_ref.3) | copy-start | bytes 6148
  212.9 13.8 %copy-start.25 = (f32[1,3,16,512]{3,2,1,0:T(8,128)S(1)}, f32[1,3,16,512]{3,2,1,0:T(8,128)}, u32[]{:S(2)}) copy-start(f32[1,3,16,512]{3,2,1,0:T(8,128)} %param.16) | copy-start | bytes 294916
  212.9 13.8 %copy-start.26 = (f32[1,3,16,512]{3,2,1,0:T(8,128)S(1)}, f32[1,3,16,512]{3,2,1,0:T(8,128)}, u32[]{:S(2)}) copy-start(f32[1,3,16,512]{3,2,1,0:T(8,128)} %param.17) | copy-start | bytes 294916

commit v4 on v3

--- a/solution.py
+++ b/solution.py
@@ -76,10 +76,22 @@
 
 
 def inner_kernel(
-    seq_ref, k_ref, v_ref, r_ref, w_ref,
-    parts_ref, p1_ref, p3_ref, b_ref, own_ref, w_s, f_s, d1, d3, d2,
+    seq_ref, k_hbm, v_hbm, r_hbm, w_hbm,
+    parts_ref, p1_ref, p3_ref, b_ref, own_ref, tails_ref, f_s,
+    w_s, d1, d3, d2, k_ref, v_ref, r_ref, w_ref, sems,
 ):
+    inputs = ((k_hbm, k_ref), (w_hbm, w_ref), (r_hbm, r_ref), (v_hbm, v_ref))
+    fetches = [
+        pltpu.make_async_copy(source, target, sems.at[number])
+        for number, (source, target) in enumerate(inputs)
+    ]
+    for fetch in fetches:
+        fetch.start()
+    for fetch in fetches:
+        fetch.wait()
     tokens, dim = k_ref.shape
+    tails_ref[0] = k_ref[tokens - WIN :, :]
+    tails_ref[1] = v_ref[tokens - WIN :, :]
     scale = dim ** (-0.5)
     own = pl.ds(pl.multiple_of(seq_ref[0] * ROWS, ROWS), ROWS)
     for m in range(3):
@@ -176,11 +188,10 @@
     put_grad(parts_ref, 2, e_s, a_s)
 
 
-def second_kernel(got_ref, k_ref, v_ref, r_ref, p1_ref, p3_ref, b_ref, parts_ref, w_s, f_s, d1, d3, d2):
+def second_kernel(got_ref, k_ref, v_ref, f_s, p1_ref, p3_ref, b_ref, parts_ref, w_s, d1, d3, d2):
     tokens, dim = k_ref.shape
     scale = dim ** (-0.5)
     take_matrices(got_ref, w_s)
-    f_s[...] = columns(r_ref[...] * (-scale))
 
     def body(at):
         factor = f_s[at, :][:, :1]
@@ -237,16 +248,19 @@
     out_ref[...] = copies(d_moved.astype(bf16), NH)
 
 
-def called(kernel, outs, scratch, *args):
+def place(arg, inputs_stay):
+    if arg.dtype == jnp.int32:
+        return pl.BlockSpec(memory_space=pltpu.SMEM)
+    return pl.BlockSpec(memory_space=pltpu.HBM if inputs_stay else pltpu.VMEM)
+
+
+def called(kernel, outs, scratch, *args, inputs_stay=False):
     return pl.pallas_call(
         kernel,
         out_shape=outs,
-        in_specs=[
-            pl.BlockSpec(memory_space=pltpu.SMEM if arg.dtype == jnp.int32 else pltpu.VMEM)
-            for arg in args
-        ],
+        in_specs=[place(arg, inputs_stay) for arg in args],
         out_specs=[pl.BlockSpec(memory_space=pltpu.VMEM)] * len(outs),
-        scratch_shapes=[pltpu.VMEM(*item) for item in scratch],
+        scratch_shapes=[pltpu.VMEM(*item) if isinstance(item, tuple) else item for item in scratch],
         compiler_params=pltpu.CompilerParams(vmem_limit_bytes=VMEM_BYTES),
     )(*args)
 
@@ -288,15 +302,15 @@
     alike = pltpu.VMEM((NH, 3 * ROWS, dim), bf16)
     gain_row = gain[None, :]
 
+    parts, first_pre, third_pre, back, own, tails, factors = called(
+        inner_kernel, [owned, far, far, far, rows, pltpu.VMEM((2, WIN, dim), bf16), pltpu.VMEM(*side)],
+        [mats, half, half, half, half, half, ((1, tokens), f32), (mats[0], f32),
+         pltpu.SemaphoreType.DMA((4,))],
+        seq, *(pltpu.with_memory_space_constraint(a, pltpu.HBM) for a in (keys, values, rates, fast_init[0])),
+        inputs_stay=True,
+    )
     last = NY * NP - 1
-    pairs = [(i, i + 1) for i in range(last)]
-    tails = jnp.stack([keys[tokens - WIN :], values[tokens - WIN :]])
-    tails = lax.ppermute(tails, SEQ, pairs)
-
-    parts, first_pre, third_pre, back, own = called(
-        inner_kernel, [owned, far, far, far, rows], [mats, side, half, half, half],
-        seq, keys, values, rates, fast_init[0],
-    )
+    tails = lax.ppermute(tails, SEQ, [(i, i + 1) for i in range(last)])
     got = reduce_rows(parts)
     moved, out = called(moved_kernel, [rows, alike], [], near(got), near(own))
     renormed = gather_rows(out)
@@ -318,8 +332,8 @@
     direction = gather_rows(out)
 
     (parts,) = called(
-        second_kernel, [owned], [mats, side, half, half, half],
-        near(direction), keys, values, rates, first_pre, third_pre, back,
+        second_kernel, [owned], [mats, half, half, half],
+        near(direction), keys, values, near(factors), first_pre, third_pre, back,
     )
     grad_rows = part - totals(reduce_rows(parts))
     shape = first_moment[0].shape

time: 230 us -> 229 us (level)
  local copies, waits for them, and re-layouts: 16.8 us -> 14 us
  Pallas kernels: 16 us -> 18.3 us
    unnamed x54 -> x50, local copies, waits for them, and re-layouts: 15.3 us -> 12.6 us
where the time goes in v4:
time: 229 us; the launch traced here: 227 us
  blocking collectives  159 us (69%)
  waiting for transfers between devices  20.4 us (9%)
  Pallas kernels  18.3 us (8%)
  local copies, waits for them, and re-layouts  14 us (6%)
  starting transfers between devices  13.6 us (6%)
    all_to_all x9, blocking collectives, swapped(): return lax.all_to_all(parts, axes, split_axis=0, concat_axis=0, tiled=True)  159 us
    all_to_all x2, waiting for transfers between devices, swapped(): return lax.all_to_all(parts, axes, split_axis=0, concat_axis=0, tiled=True)  20.4 us
    pallas_call x9, Pallas kernels, called(): pl.pallas_call(kernel, out_shape=outs, in_specs=[place(arg, inputs_stay)...  18.3 us
    unnamed x50, local copies, waits for them, and re-layouts  12.6 us
    all_to_all x2, starting transfers between devices, swapped(): return lax.all_to_all(parts, axes, split_axis=0, concat_axis=0, tiled=True)  10.1 us
  transfers between devices with their start and end apart: 3, of which 2 were waited for; matrix products, arithmetic and copies ran while one was open for 0% of the time, Pallas kernels for 1%

profile of v4, /device:TPU:24, one launch (start us, length us, event | category | flops | bytes accessed | tf_op | source)
XLA Modules:
  0.0 227.0 jit_solution(9434679594642969981)
XLA Ops:
  0.6 5.3 %shard_map.120 = (bf16[8,192,512]{2,1,0:T(8,128)(2,1)S(1)}, f32[512,512]{1,0:T(8,128)S(1)}, f32[512,512]{1,0:T(8,128)S(1)}, f32[512,512]{1,0:T(8,128)S(1)}, f32[...) custom-call(s32[1]{0:T(128)} %bitcast.seq_ref, bf16[512,512]{1,0:T(8,128)(2,1)} %k_ref.3, ...), custom_call_target="tpu_custom_call" | custom-call | tf_op jit(solution)/shard_map/pallas_call | solution.py:258
  5.9 1.0 copy-done.11
  6.9 1.0 copy-done.13
  7.9 24.9 %all_to_all.55.got_ref = bf16[8,192,512]{2,1,0:T(8,128)(2,1)S(1)} all-to-all(bf16[8,192,512]{2,1,0:T(8,128)(2,1)S(1)} %get-tuple-element.22), channel_id=1, replica_groups=mesh['zh'=4,'zl'=2,'y'=4,'x'=4,'c'=2] {'zl','y'}, dimensions={0} | all-to-all | bytes 3145728 | tf_op jit(solution)/shard_map/all_to_all | solution.py:35
  33.0 16.8 %all_to_all.56.got_ref = bf16[4,48,512]{2,1,0:T(8,128)(2,1)S(1)} all-to-all(bf16[4,48,512]{2,1,0:T(8,128)(2,1)S(1)} %shard_map.121), channel_id=1, replica_groups=mesh['zh'=4,'zl'=2,'y'=4,'x'=4,'c'=2] {'zh'}, dimensions={0} | all-to-all | bytes 393216 | tf_op jit(solution)/shard_map/all_to_all | solution.py:35
  50.0 11.4 %all_to_all.57 = bf16[4,48,512]{2,1,0:T(8,128)(2,1)S(1)} all-to-all(bf16[4,48,512]{2,1,0:T(8,128)(2,1)S(1)} %get-tuple-element.24), channel_id=1, replica_groups=mesh['zh'=4,'zl'=2,'y'=4,'x'=4,'c'=2] {'zh'}, dimensions={0} | all-to-all | bytes 393216 | tf_op jit(solution)/shard_map/all_to_all | solution.py:35
  61.4 1.3 broadcast_in_dim.12
  62.7 5.8 %all-to-all-start.3 = ((bf16[8,192,512]{2,1,0:T(8,128)(2,1)}), bf16[8,192,512]{2,1,0:T(8,128)(2,1)S(1)}, u32[]{:S(2)}, u32[]{:S(2)}) async-start(bf16[8,192,512]{2,1,0:T(8,128)(2,1)} %broadcast_in_dim.12), calls=%async_computation.3 | async-start | bytes 3145728 | tf_op jit(solution)/shard_map/all_to_all | solution.py:35
  68.5 3.5 %collective-permute-start = (bf16[2,256,512]{2,1,0:T(8,128)(2,1)}, bf16[2,256,512]{2,1,0:T(8,128)(2,1)}, u32[]{:S(2)}, u32[]{:S(2)}) collective-permute-start(bf16[2,256,512]{2,1,0:T(8,128)(2,1)} %copy-done.22), channel_id=1, source_target_pairs={{0,8},{8,16},{16,24},{24,32},{32,40},{40,48},{48,56},{56,64},{64,7... | collective-permute-start | bytes 1572872 | tf_op jit(solution)/shard_map/ppermute | solution.py:313
  72.0 14.9 %all-to-all-done.3.got_ref = bf16[8,192,512]{2,1,0:T(8,128)(2,1)S(1)} async-done(((bf16[8,192,512]{2,1,0:T(8,128)(2,1)}), bf16[8,192,512]{2,1,0:T(8,128)(2,1)S(1)}, u32[]{:S(2)}, u32[]{:S(2)}) %all-to-all-start.3) | async-done | bytes 1572896 | tf_op jit(solution)/shard_map/all_to_all | solution.py:35
  86.9 1.0 copy-done.3
  87.9 3.3 %shard_map.123 = (f32[512,512]{1,0:T(8,128)S(1)}, f32[512,512]{1,0:T(8,128)S(1)}, f32[512,512]{1,0:T(8,128)S(1)}, f32[8,2,512]{2,1,0:T(2,128)}, bf16[512,512]{1,0:T(8,128)(2,1)S(1)}) custom-call(bf16[8,192,512]{2,1,0:T(8,128)(2,1)S(1)} %all-to-all-done.3.got_ref, bf16[512,512]{1,0:T(8,128)(2,1)S(1)} %copy-done.2, bf16[512,512]{1,0:T(8,128)(2,1)S(1)} %copy-done.3, ...), custom_call_target="tpu_custom_call" | custom-call | tf_op jit(solution)/shard_map/pallas_call | solution.py:258
  91.3 1.0 copy-done.5
  92.3 1.0 copy-done.7
  93.3 1.0 copy-done.9
  94.3 0.8 copy-done.17
  95.1 4.3 %all-to-all-start.4 = ((f32[8,2,512]{2,1,0:T(2,128)}), f32[8,2,512]{2,1,0:T(2,128)S(1)}, u32[]{:S(2)}, u32[]{:S(2)}) async-start(f32[8,2,512]{2,1,0:T(2,128)} %get-tuple-element.25), calls=%async_computation.4 | async-start | bytes 65536 | tf_op jit(solution)/shard_map/all_to_all | solution.py:35
  99.4 5.4 %all-to-all-done.4.sums_ref = f32[8,2,512]{2,1,0:T(2,128)S(1)} async-done(((f32[8,2,512]{2,1,0:T(2,128)}), f32[8,2,512]{2,1,0:T(2,128)S(1)}, u32[]{:S(2)}, u32[]{:S(2)}) %all-to-all-start.4) | async-done | bytes 32800 | tf_op jit(solution)/shard_map/all_to_all | solution.py:35
  104.8 1.0 copy-done.4
  105.9 1.2 copy-done.6
  107.1 1.2 copy-done.8
  108.3 1.2 copy-done.10
  109.5 1.0 copy-done.18
  110.6 5.5 %shard_map.124 = (bf16[8,192,512]{2,1,0:T(8,128)(2,1)S(1)}, bf16[512,512]{1,0:T(8,128)(2,1)}) custom-call(s32[1]{0:T(128)} %bitcast.seq_ref, f32[8,2,512]{2,1,0:T(2,128)S(1)} %all-to-all-done.4.sums_ref, f32[512,512]{1,0:T(8,128)S(1)} %copy-done.6, f32[512,512]{1,0:T(8,128)S(1)} %copy-done.8, f32[512,512]{1,0:T(8,128)S(1)} %copy-done.10, ...), custom_call_target="tpu_custom_call" | custom-call | tf_op jit(solution)/shard_map/pallas_call | solution.py:258
  116.1 25.1 %all_to_all.58.got_ref = bf16[8,192,512]{2,1,0:T(8,128)(2,1)S(1)} all-to-all(bf16[8,192,512]{2,1,0:T(8,128)(2,1)S(1)} %get-tuple-element.32), channel_id=1, replica_groups=mesh['zh'=4,'zl'=2,'y'=4,'x'=4,'c'=2] {'zl','y'}, dimensions={0} | all-to-all | bytes 3145728 | tf_op jit(solution)/shard_map/all_to_all | solution.py:35
  141.5 17.4 %all_to_all.59.got_ref = bf16[4,48,512]{2,1,0:T(8,128)(2,1)S(1)} all-to-all(bf16[4,48,512]{2,1,0:T(8,128)(2,1)S(1)} %shard_map.125), channel_id=1, replica_groups=mesh['zh'=4,'zl'=2,'y'=4,'x'=4,'c'=2] {'zh'}, dimensions={0} | all-to-all | bytes 393216 | tf_op jit(solution)/shard_map/all_to_all | solution.py:35
  159.0 11.5 %all_to_all.60 = bf16[4,48,512]{2,1,0:T(8,128)(2,1)S(1)} all-to-all(bf16[4,48,512]{2,1,0:T(8,128)(2,1)S(1)} %get-tuple-element.35), channel_id=1, replica_groups=mesh['zh'=4,'zl'=2,'y'=4,'x'=4,'c'=2] {'zh'}, dimensions={0} | all-to-all | bytes 393216 | tf_op jit(solution)/shard_map/all_to_all | solution.py:35
  170.6 20.2 %all_to_all.61.got_ref = bf16[8,192,512]{2,1,0:T(8,128)(2,1)S(1)} all-to-all(bf16[8,192,512]{2,1,0:T(8,128)(2,1)S(1)} %broadcast_in_dim.14), channel_id=1, replica_groups=mesh['zh'=4,'zl'=2,'y'=4,'x'=4,'c'=2] {'zl','y'}, dimensions={0} | all-to-all | bytes 3145728 | tf_op jit(solution)/shard_map/all_to_all | solution.py:35
  190.8 3.3 %shard_map.127 = bf16[8,192,512]{2,1,0:T(8,128)(2,1)S(1)} custom-call(bf16[8,192,512]{2,1,0:T(8,128)(2,1)S(1)} %all_to_all.61.got_ref, bf16[512,512]{1,0:T(8,128)(2,1)S(1)} %copy-done, bf16[512,512]{1,0:T(8,128)(2,1)S(1)} %copy-done.1, f32[512,128]{1,0:T(8,128)S(1)} %get-tuple-element.36.f_s, f32[512,512]{1,0:T(8,128)S(1)} %copy-done.12, ...), custom_call_target="tpu_custom_call" | custom-call | tf_op jit(solution)/shard_map/pallas_call | solution.py:258
  194.1 18.3 %all_to_all.62.got_ref = bf16[8,192,512]{2,1,0:T(8,128)(2,1)S(1)} all-to-all(bf16[8,192,512]{2,1,0:T(8,128)(2,1)S(1)} %shard_map.127), channel_id=1, replica_groups=mesh['zh'=4,'zl'=2,'y'=4,'x'=4,'c'=2] {'zl','y'}, dimensions={0} | all-to-all | bytes 3145728 | tf_op jit(solution)/shard_map/all_to_all | solution.py:35
  212.6 13.5 %all_to_all.63 = bf16[4,48,512]{2,1,0:T(8,128)(2,1)S(1)} all-to-all(bf16[4,48,512]{2,1,0:T(8,128)(2,1)S(1)} %shard_map.128), channel_id=1, replica_groups=mesh['zh'=4,'zl'=2,'y'=4,'x'=4,'c'=2] {'zh'}, dimensions={0} | all-to-all | bytes 393216 | tf_op jit(solution)/shard_map/all_to_all | solution.py:35
  226.2 0.7 divide_subtract_fusion
  (47 shorter events, 1.1 us)
Async XLA Ops:
  5.9 1.0 copy-start.11
  6.9 1.0 copy-start.13
  7.9 24.9 %copy-start.15 = (f32[512,512]{1,0:T(8,128)}, f32[512,512]{1,0:T(8,128)S(1)}, u32[]{:S(2)}) copy-start(f32[512,512]{1,0:T(8,128)S(1)} %get-tuple-element.39.b_ref) | copy-start | bytes 3145732
  7.9 24.9 %copy-start.22 = (bf16[2,256,512]{2,1,0:T(8,128)(2,1)}, bf16[2,256,512]{2,1,0:T(8,128)(2,1)S(1)}, u32[]{:S(2)}) copy-start(bf16[2,256,512]{2,1,0:T(8,128)(2,1)S(1)} %get-tuple-element.30) | copy-start | bytes 1572868
  49.9 11.5 %copy-start.19 = (f32[48,512]{1,0:T(8,128)}, f32[48,512]{1,0:T(8,128)S(1)}, u32[]{:S(2)}) copy-start(f32[48,512]{1,0:T(8,128)S(1)} %get-tuple-element.33.moved_ref) | copy-start | bytes 294916
  62.7 24.2 %copy-start.2 = (bf16[512,512]{1,0:T(8,128)(2,1)S(1)}, bf16[512,512]{1,0:T(8,128)(2,1)}, u32[]{:S(2)}) copy-start(bf16[512,512]{1,0:T(8,128)(2,1)} %q_ref.3) | copy-start | bytes 1572868
  62.7 24.2 %copy-start.21 = (f32[512]{0:T(512)S(1)}, f32[512]{0:T(512)}, u32[]{:S(2)}) copy-start(f32[512]{0:T(512)} %param.13) | copy-start | bytes 6148
  62.7 24.2 %all-to-all-start.3 = ((bf16[8,192,512]{2,1,0:T(8,128)(2,1)}), bf16[8,192,512]{2,1,0:T(8,128)(2,1)S(1)}, u32[]{:S(2)}, u32[]{:S(2)}) async-start(bf16[8,192,512]{2,1,0:T(8,128)(2,1)} %broadcast_in_dim.12), calls=%async_computation.3 | async-start | bytes 3145728 | tf_op jit(solution)/shard_map/all_to_all | solution.py:35
  68.5 36.4 %copy-start = (bf16[512,512]{1,0:T(8,128)(2,1)S(1)}, bf16[512,512]{1,0:T(8,128)(2,1)}, u32[]{:S(2)}) copy-start(bf16[512,512]{1,0:T(8,128)(2,1)} %k_ref.3) | copy-start | bytes 1572868
  68.5 36.4 %copy-start.1 = (bf16[512,512]{1,0:T(8,128)(2,1)S(1)}, bf16[512,512]{1,0:T(8,128)(2,1)}, u32[]{:S(2)}) copy-start(bf16[512,512]{1,0:T(8,128)(2,1)} %v_ref.3) | copy-start | bytes 1572868
  68.5 30.9 %collective-permute-start = (bf16[2,256,512]{2,1,0:T(8,128)(2,1)}, bf16[2,256,512]{2,1,0:T(8,128)(2,1)}, u32[]{:S(2)}, u32[]{:S(2)}) collective-permute-start(bf16[2,256,512]{2,1,0:T(8,128)(2,1)} %copy-done.22), channel_id=1, source_target_pairs={{0,8},{8,16},{16,24},{24,32},{32,40},{40,48},{48,56},{56,64},{64,7... | collective-permute-start | bytes 1572872 | tf_op jit(solution)/shard_map/ppermute | solution.py:313
  86.9 1.0 copy-start.3
  91.3 1.0 copy-start.5
  92.3 1.0 copy-start.7
  93.3 1.0 copy-start.9
  94.3 0.8 copy-start.17
  95.1 9.8 %all-to-all-start.4 = ((f32[8,2,512]{2,1,0:T(2,128)}), f32[8,2,512]{2,1,0:T(2,128)S(1)}, u32[]{:S(2)}, u32[]{:S(2)}) async-start(f32[8,2,512]{2,1,0:T(2,128)} %get-tuple-element.25), calls=%async_computation.4 | async-start | bytes 65536 | tf_op jit(solution)/shard_map/all_to_all | solution.py:35
  104.8 1.0 copy-start.4
  105.9 1.2 copy-start.6
  107.1 1.2 copy-start.8
  108.3 1.2 copy-start.10
  109.5 1.0 copy-start.18
  141.3 17.6 %copy-start.20 = (f32[48,512]{1,0:T(8,128)S(1)}, f32[48,512]{1,0:T(8,128)}, u32[]{:S(2)}) copy-start(f32[48,512]{1,0:T(8,128)} %copy-done.19) | copy-start | bytes 294916
  170.6 20.2 %copy-start.12 = (f32[512,512]{1,0:T(8,128)S(1)}, f32[512,512]{1,0:T(8,128)}, u32[]{:S(2)}) copy-start(f32[512,512]{1,0:T(8,128)} %copy-done.11) | copy-start | bytes 3145732
  170.6 20.2 %copy-start.14 = (f32[512,512]{1,0:T(8,128)S(1)}, f32[512,512]{1,0:T(8,128)}, u32[]{:S(2)}) copy-start(f32[512,512]{1,0:T(8,128)} %copy-done.13) | copy-start | bytes 3145732
  170.6 20.2 %copy-start.16 = (f32[512,512]{1,0:T(8,128)S(1)}, f32[512,512]{1,0:T(8,128)}, u32[]{:S(2)}) copy-start(f32[512,512]{1,0:T(8,128)} %copy-done.15) | copy-start | bytes 3145732
  212.4 13.8 %copy-start.23 = (f32[1,3,16,512]{3,2,1,0:T(8,128)S(1)}, f32[1,3,16,512]{3,2,1,0:T(8,128)}, u32[]{:S(2)}) copy-start(f32[1,3,16,512]{3,2,1,0:T(8,128)} %param.16) | copy-start | bytes 294916
  212.4 13.8 %copy-start.24 = (f32[1,3,16,512]{3,2,1,0:T(8,128)S(1)}, f32[1,3,16,512]{3,2,1,0:T(8,128)}, u32[]{:S(2)}) copy-start(f32[1,3,16,512]{3,2,1,0:T(8,128)} %param.17) | copy-start | bytes 294916

commit v5 on v4

--- a/solution.py
+++ b/solution.py
@@ -80,33 +80,41 @@
     parts_ref, p1_ref, p3_ref, b_ref, own_ref, tails_ref, f_s,
     w_s, d1, d3, d2, k_ref, v_ref, r_ref, w_ref, sems,
 ):
-    inputs = ((k_hbm, k_ref), (w_hbm, w_ref), (r_hbm, r_ref), (v_hbm, v_ref))
+    inputs = [(k_hbm, k_ref)] + [(w_hbm.at[m], w_ref.at[m]) for m in range(3)]
+    inputs += [(v_hbm, v_ref), (r_hbm, r_ref)]
     fetches = [
         pltpu.make_async_copy(source, target, sems.at[number])
         for number, (source, target) in enumerate(inputs)
     ]
     for fetch in fetches:
         fetch.start()
-    for fetch in fetches:
+    tokens, dim = k_ref.shape
+    scale = dim ** (-0.5)
+    for fetch in fetches[:3]:
         fetch.wait()
-    tokens, dim = k_ref.shape
+    w_s[0] = w_ref[0].astype(bf16)
+    w_s[1] = w_ref[1].astype(bf16)
+
+    def first(at):
+        p1_ref[at, :] = scale * mm(k_ref[at, :], w_s[0], 1, 0)
+        p3_ref[at, :] = scale * mm(k_ref[at, :], w_s[1], 1, 0)
+
+    blocks_of(tokens, first)
+    for fetch in fetches[3:]:
+        fetch.wait()
+    w_s[2] = w_ref[2].astype(bf16)
     tails_ref[0] = k_ref[tokens - WIN :, :]
     tails_ref[1] = v_ref[tokens - WIN :, :]
-    scale = dim ** (-0.5)
     own = pl.ds(pl.multiple_of(seq_ref[0] * ROWS, ROWS), ROWS)
     for m in range(3):
-        w_s[m] = w_ref[m].astype(bf16)
         own_ref[m * ROWS : (m + 1) * ROWS, :] = w_ref[m, own, :]
     f_s[...] = columns(r_ref[...] * (-scale))
 
     def body(at):
         factor = f_s[at, :][:, :1]
-        p1 = scale * mm(k_ref[at, :], w_s[0], 1, 0)
-        p3 = scale * mm(k_ref[at, :], w_s[1], 1, 0)
+        p3 = p3_ref[at, :]
         back = factor * mm(v_ref[at, :], w_s[2], 1, 0)
-        gate, gate1, _ = gates(p1)
-        p1_ref[at, :] = p1
-        p3_ref[at, :] = p3
+        gate, gate1, _ = gates(p1_ref[at, :])
         b_ref[at, :] = back
         d1[at, :] = (scale * back * p3 * gate1).astype(bf16)
         d3[at, :] = (scale * back * gate).astype(bf16)
@@ -143,10 +151,42 @@
 
 
 def backward_kernel(
-    seq_ref, sums_ref, o_ref, p1_ref, p3_ref, q_ref, cot_ref, gain_ref, w2_ref, k_ref, v_ref, tails_ref,
-    parts_ref, layer_ref, s_s, d1, d3, a_s, e_s, all_s,
+    sums_ref, o_ref, p1_ref, p3_ref, q_ref, cot_ref, gain_ref, w2_ref,
+    parts_ref, normed_ref, s_s, d1, d3, a_s, e_s,
 ):
     tokens, dim = q_ref.shape
+    scale = dim ** (-0.5)
+    sums = jnp.sum(sums_ref[...], axis=0)
+    inverse = 1.0 / jnp.sqrt(sums[:1] / WIDTH + 1e-06)
+    coef = sums[1:] * inverse * inverse * inverse / WIDTH
+    s_s[0] = columns(inverse)
+    s_s[1] = columns(coef)
+
+    def body(at):
+        inv = s_s[0, at, :][:, :1]
+        out = o_ref[at, :]
+        weighted = cot_ref[at, :].astype(f32) * gain_ref[...]
+        err = (scale * (weighted * inv - out * s_s[1, at, :][:, :1])).astype(bf16)
+        e_s[at, :] = err
+        normed_ref[at, :] = out * inv * gain_ref[...]
+        back = mm(err, w2_ref[...], 1, 0)
+        p3 = p3_ref[at, :]
+        gate, gate1, _ = gates(p1_ref[at, :])
+        d1[at, :] = (scale * back * p3 * gate1).astype(bf16)
+        d3[at, :] = (scale * back * gate).astype(bf16)
+        a_s[at, :] = (gate * p3).astype(bf16)
+
+    blocks_of(tokens, body)
+    put_grad(parts_ref, 0, q_ref, d1)
+    put_grad(parts_ref, 1, q_ref, d3)
+    put_grad(parts_ref, 2, e_s, a_s)
+
+
+def second_kernel(
+    seq_ref, got_ref, k_ref, v_ref, f_s, p1_ref, p3_ref, b_ref, q_ref, normed_ref, tails_ref,
+    parts_ref, layer_ref, w_s, d1, d3, d2, all_s,
+):
+    tokens, dim = k_ref.shape
     scale = dim ** (-0.5)
     all_s[:, :WIN, :] = tails_ref[...]
     all_s[0, WIN:, :] = k_ref[...]
@@ -155,42 +195,6 @@
     ahead = lax.broadcasted_iota(jnp.int32, (BLOCK, span), 1)
     behind = ahead - lax.broadcasted_iota(jnp.int32, (BLOCK, span), 0)
     near_by = (behind > 0) & (behind <= WIN)
-    sums = jnp.sum(sums_ref[...], axis=0)
-    inverse = 1.0 / jnp.sqrt(sums[:1] / WIDTH + 1e-06)
-    coef = sums[1:] * inverse * inverse * inverse / WIDTH
-    s_s[0] = columns(inverse)
-    s_s[1] = columns(coef)
-
-    def body(at):
-        inv = s_s[0, at, :][:, :1]
-        out = o_ref[at, :]
-        weighted = cot_ref[at, :].astype(f32) * gain_ref[...]
-        err = (scale * (weighted * inv - out * s_s[1, at, :][:, :1])).astype(bf16)
-        e_s[at, :] = err
-        window = pl.ds(at.start, span)
-        scores = scale * mm(q_ref[at, :], all_s[0, window, :], 1, 1)
-        known = near_by & (ahead + (seq_ref[0] * tokens + at.start) >= WIN)
-        scores = jnp.where(known, scores, -1e30)
-        expo = jnp.exp(scores - jnp.max(scores, axis=1, keepdims=True))
-        probs = expo / jnp.sum(expo, axis=1, keepdims=True)
-        attention = mm(probs, all_s[1, window, :], 1, 0)
-        layer_ref[at, :] = (attention + out * inv * gain_ref[...]).astype(bf16)
-        back = mm(err, w2_ref[...], 1, 0)
-        p3 = p3_ref[at, :]
-        gate, gate1, _ = gates(p1_ref[at, :])
-        d1[at, :] = (scale * back * p3 * gate1).astype(bf16)
-        d3[at, :] = (scale * back * gate).astype(bf16)
-        a_s[at, :] = (gate * p3).astype(bf16)
-
-    blocks_of(tokens, body)
-    put_grad(parts_ref, 0, q_ref, d1)
-    put_grad(parts_ref, 1, q_ref, d3)
-    put_grad(parts_ref, 2, e_s, a_s)
-
-
-def second_kernel(got_ref, k_ref, v_ref, f_s, p1_ref, p3_ref, b_ref, parts_ref, w_s, d1, d3, d2):
-    tokens, dim = k_ref.shape
-    scale = dim ** (-0.5)
     take_matrices(got_ref, w_s)
 
     def body(at):
@@ -208,6 +212,14 @@
         ).astype(bf16)
         d3[at, :] = (scale * (back_dot * gate + back * bent)).astype(bf16)
         d2[at, :] = (factor * (bent * p3 + gate * third_dot)).astype(bf16)
+        window = pl.ds(at.start, span)
+        scores = scale * mm(q_ref[at, :], all_s[0, window, :], 1, 1)
+        known = near_by & (ahead + (seq_ref[0] * tokens + at.start) >= WIN)
+        scores = jnp.where(known, scores, -1e30)
+        expo = jnp.exp(scores - jnp.max(scores, axis=1, keepdims=True))
+        probs = expo / jnp.sum(expo, axis=1, keepdims=True)
+        attention = mm(probs, all_s[1, window, :], 1, 0)
+        layer_ref[at, :] = (attention + normed_ref[at, :]).astype(bf16)
 
     blocks_of(tokens, body)
     put_grad(parts_ref, 0, k_ref, d1)
@@ -274,7 +286,8 @@
 
 def gather_rows(rows):
     some = swapped(rows, "zh")
-    return swapped(copies(some.reshape(-1, rows.shape[2]), NP), PLANE)
+    some = copies(some.reshape(-1, rows.shape[2]), NP)
+    return swapped(some, PLANE)
 
 
 def adam_step(weights, gradient, first_moment, second_moment):
@@ -305,7 +318,7 @@
     parts, first_pre, third_pre, back, own, tails, factors = called(
         inner_kernel, [owned, far, far, far, rows, pltpu.VMEM((2, WIN, dim), bf16), pltpu.VMEM(*side)],
         [mats, half, half, half, half, half, ((1, tokens), f32), (mats[0], f32),
-         pltpu.SemaphoreType.DMA((4,))],
+         pltpu.SemaphoreType.DMA((6,))],
         seq, *(pltpu.with_memory_space_constraint(a, pltpu.HBM) for a in (keys, values, rates, fast_init[0])),
         inputs_stay=True,
     )
@@ -321,19 +334,20 @@
         near(renormed), queries, cotangent, gain_row,
     )
     sums = swapped(sums, HEAD)
-    parts, layer_out = called(
-        backward_kernel, [owned, jax.ShapeDtypeStruct(*half)],
-        [((2, tokens, 128), f32), half, half, half, half, ((2, tokens + WIN, dim), bf16)],
-        seq, near(sums), near(fast_out), near(first_q), near(third_q), queries, cotangent, gain_row,
-        near(second_w), keys, values, tails,
+    parts, normed = called(
+        backward_kernel, [owned, full], [((2, tokens, 128), f32), half, half, half, half],
+        near(sums), near(fast_out), near(first_q), near(third_q), queries, cotangent, gain_row,
+        near(second_w),
     )
     got = reduce_rows(parts)
     part, out = called(pulled_kernel, [rows, alike], [], near(got), near(own), near(moved))
     direction = gather_rows(out)
 
-    (parts,) = called(
-        second_kernel, [owned], [mats, half, half, half],
-        near(direction), keys, values, near(factors), first_pre, third_pre, back,
+    parts, layer_out = called(
+        second_kernel, [owned, jax.ShapeDtypeStruct(*half)],
+        [mats, half, half, half, ((2, tokens + WIN, dim), bf16)],
+        seq, near(direction), keys, values, near(factors), first_pre, third_pre, back, queries,
+        near(normed), near(tails),
     )
     grad_rows = part - totals(reduce_rows(parts))
     shape = first_moment[0].shape

time: 229 us -> 229 us (level)
  blocking collectives: 159 us -> 167 us
  starting transfers between devices: 13.6 us -> 9.25 us
  local copies, waits for them, and re-layouts: 14 us -> 11.2 us
    ppermute x1, waiting for transfers between devices: 0.01 us -> 22 us  [inner_local(): tails = lax.ppermute(tails, SEQ, [(i, i + 1) for i in range(last)])]
    all_to_all x2 -> x1, waiting for transfers between devices: 20.4 us -> 0.01 us  [swapped(): return lax.all_to_all(parts, axes, split_axis=0, concat_axis=0, tiled=True)]
    all_to_all x9 -> x10, blocking collectives: 159 us -> 167 us  [swapped(): return lax.all_to_all(parts, axes, split_axis=0, concat_axis=0, tiled=True)]
    all_to_all x2 -> x1, starting transfers between devices: 10.1 us -> 5.89 us  [swapped(): return lax.all_to_all(parts, axes, split_axis=0, concat_axis=0, tiled=True)]
    unnamed x50 -> x40, local copies, waits for them, and re-layouts: 12.6 us -> 9.72 us
  transfers between devices with their start and end apart: 3 -> 2, of which waited for: 2 -> 1; matrix products, arithmetic and copies ran while one was open for 0% -> 0% of each run, Pallas kernels for 1% -> 0%
where the time goes in v5:
time: 229 us; the launch traced here: 228 us
  blocking collectives  167 us (73%)
  waiting for transfers between devices  22.1 us (10%)
  Pallas kernels  17.1 us (7%)
  local copies, waits for them, and re-layouts  11.2 us (5%)
  starting transfers between devices  9.25 us (4%)
    all_to_all x10, blocking collectives, swapped(): return lax.all_to_all(parts, axes, split_axis=0, concat_axis=0, tiled=True)  167 us
    ppermute x1, waiting for transfers between devices, inner_local(): tails = lax.ppermute(tails, SEQ, [(i, i + 1) for i in range(last)])  22 us
    pallas_call x9, Pallas kernels, called(): pl.pallas_call(kernel, out_shape=outs, in_specs=[place(arg, inputs_stay)...  17.1 us
    unnamed x40, local copies, waits for them, and re-layouts  9.72 us
    all_to_all x1, starting transfers between devices, swapped(): return lax.all_to_all(parts, axes, split_axis=0, concat_axis=0, tiled=True)  5.89 us
  transfers between devices with their start and end apart: 2, of which 1 were waited for; matrix products, arithmetic and copies ran while one was open for 0% of the time, Pallas kernels for 0%

profile of v5, /device:TPU:24, one launch (start us, length us, event | category | flops | bytes accessed | tf_op | source)
XLA Modules:
  0.0 227.8 jit_solution(17060231103834010147)
XLA Ops:
  0.6 5.5 %shard_map.120 = (bf16[8,192,512]{2,1,0:T(8,128)(2,1)S(1)}, f32[512,512]{1,0:T(8,128)S(1)}, f32[512,512]{1,0:T(8,128)S(1)}, f32[512,512]{1,0:T(8,128)S(1)}, f32[...) custom-call(s32[1]{0:T(128)} %bitcast.seq_ref, bf16[512,512]{1,0:T(8,128)(2,1)} %k_ref.1, ...), custom_call_target="tpu_custom_call" | custom-call | tf_op jit(solution)/shard_map/pallas_call | solution.py:270
  6.2 1.0 copy-done.4
  7.2 1.0 copy-done.6
  8.2 24.9 %all_to_all.55.got_ref = bf16[8,192,512]{2,1,0:T(8,128)(2,1)S(1)} all-to-all(bf16[8,192,512]{2,1,0:T(8,128)(2,1)S(1)} %get-tuple-element.24), channel_id=1, replica_groups=mesh['zh'=4,'zl'=2,'y'=4,'x'=4,'c'=2] {'zl','y'}, dimensions={0} | all-to-all | bytes 3145728 | tf_op jit(solution)/shard_map/all_to_all | solution.py:35
  33.0 0.2 shard_map.121
  33.3 16.8 %all_to_all.56.got_ref = bf16[4,48,512]{2,1,0:T(8,128)(2,1)S(1)} all-to-all(bf16[4,48,512]{2,1,0:T(8,128)(2,1)S(1)} %shard_map.121), channel_id=1, replica_groups=mesh['zh'=4,'zl'=2,'y'=4,'x'=4,'c'=2] {'zh'}, dimensions={0} | all-to-all | bytes 393216 | tf_op jit(solution)/shard_map/all_to_all | solution.py:35
  50.1 0.1 shard_map.122
  50.2 11.4 %all_to_all.57 = bf16[4,48,512]{2,1,0:T(8,128)(2,1)S(1)} all-to-all(bf16[4,48,512]{2,1,0:T(8,128)(2,1)S(1)} %get-tuple-element.26), channel_id=1, replica_groups=mesh['zh'=4,'zl'=2,'y'=4,'x'=4,'c'=2] {'zh'}, dimensions={0} | all-to-all | bytes 393216 | tf_op jit(solution)/shard_map/all_to_all | solution.py:35
  61.9 20.0 %all_to_all.58.got_ref = bf16[8,192,512]{2,1,0:T(8,128)(2,1)S(1)} all-to-all(bf16[8,192,512]{2,1,0:T(8,128)(2,1)S(1)} %broadcast_in_dim.12), channel_id=1, replica_groups=mesh['zh'=4,'zl'=2,'y'=4,'x'=4,'c'=2] {'zl','y'}, dimensions={0} | all-to-all | bytes 3145728 | tf_op jit(solution)/shard_map/all_to_all | solution.py:35
  81.8 2.7 %shard_map.123 = (f32[512,512]{1,0:T(8,128)S(1)}, f32[512,512]{1,0:T(8,128)S(1)}, f32[512,512]{1,0:T(8,128)S(1)}, f32[8,2,512]{2,1,0:T(2,128)S(1)}, bf16[512,512]{1,0:T(8,128)(2,1)S(1)}) custom-call(bf16[8,192,512]{2,1,0:T(8,128)(2,1)S(1)} %all_to_all.58.got_ref, bf16[512,512]{1,0:T(8,128)(2,1)S(1)} %copy-done, bf16[512,512]{1,0:T(8,128)(2,1)S(1)} %copy-done.1, ...), custom_call_target="tpu_custom_call" | custom-call | tf_op jit(solution)/shard_map/pallas_call | solution.py:270
  84.6 9.5 %all_to_all.59.sums_ref = f32[8,2,512]{2,1,0:T(2,128)S(1)} all-to-all(f32[8,2,512]{2,1,0:T(2,128)S(1)} %get-tuple-element.27), channel_id=1, replica_groups=mesh['zh'=4,'zl'=2,'y'=4,'x'=4,'c'=2] {'x','c'}, dimensions={0} | all-to-all | bytes 65536 | tf_op jit(solution)/shard_map/all_to_all | solution.py:35
  94.1 2.7 %shard_map.124 = (bf16[8,192,512]{2,1,0:T(8,128)(2,1)S(1)}, f32[512,512]{1,0:T(8,128)S(1)}) custom-call(f32[8,2,512]{2,1,0:T(2,128)S(1)} %all_to_all.59.sums_ref, f32[512,512]{1,0:T(8,128)S(1)} %get-tuple-element.28.o_ref, f32[512,512]{1,0:T(8,128)S(1)} %get-tuple-element.29.p1_ref, f32[512,512]{1,0:T(8,128)S(1)} %get-tuple-element.30.p3_ref, ...), custom_call_target="tpu_custom_call" | custom-call | tf_op jit(solution)/shard_map/pallas_call | solution.py:270
  96.9 1.0 copy-done.10
  97.9 24.1 %all_to_all.60.got_ref = bf16[8,192,512]{2,1,0:T(8,128)(2,1)S(1)} all-to-all(bf16[8,192,512]{2,1,0:T(8,128)(2,1)S(1)} %get-tuple-element.32), channel_id=1, replica_groups=mesh['zh'=4,'zl'=2,'y'=4,'x'=4,'c'=2] {'zl','y'}, dimensions={0} | all-to-all | bytes 3145728 | tf_op jit(solution)/shard_map/all_to_all | solution.py:35
  122.0 0.2 shard_map.125
  122.2 12.0 %all_to_all.61.got_ref = bf16[4,48,512]{2,1,0:T(8,128)(2,1)S(1)} all-to-all(bf16[4,48,512]{2,1,0:T(8,128)(2,1)S(1)} %shard_map.125), channel_id=1, replica_groups=mesh['zh'=4,'zl'=2,'y'=4,'x'=4,'c'=2] {'zh'}, dimensions={0} | all-to-all | bytes 393216 | tf_op jit(solution)/shard_map/all_to_all | solution.py:35
  134.3 11.4 %all_to_all.62 = bf16[4,48,512]{2,1,0:T(8,128)(2,1)S(1)} all-to-all(bf16[4,48,512]{2,1,0:T(8,128)(2,1)S(1)} %get-tuple-element.34), channel_id=1, replica_groups=mesh['zh'=4,'zl'=2,'y'=4,'x'=4,'c'=2] {'zh'}, dimensions={0} | all-to-all | bytes 393216 | tf_op jit(solution)/shard_map/all_to_all | solution.py:35
  145.8 1.3 broadcast_in_dim.14
  147.1 5.9 %all-to-all-start.8 = ((bf16[8,192,512]{2,1,0:T(8,128)(2,1)}), bf16[8,192,512]{2,1,0:T(8,128)(2,1)S(1)}, u32[]{:S(2)}, u32[]{:S(2)}) async-start(bf16[8,192,512]{2,1,0:T(8,128)(2,1)} %broadcast_in_dim.14), calls=%async_computation.8 | async-start | bytes 3145728 | tf_op jit(solution)/shard_map/all_to_all | solution.py:35
  153.0 3.4 %collective-permute-start = (bf16[2,256,512]{2,1,0:T(8,128)(2,1)}, bf16[2,256,512]{2,1,0:T(8,128)(2,1)S(1)}, u32[]{:S(2)}, u32[]{:S(2)}) collective-permute-start(bf16[2,256,512]{2,1,0:T(8,128)(2,1)} %copy-done.17), channel_id=1, source_target_pairs={{0,8},{8,16},{16,24},{24,32},{32,40},{40,48},{48,56},{56,64},{64,7... | collective-permute-start | bytes 1572872 | tf_op jit(solution)/shard_map/ppermute | solution.py:326
  156.4 22.0 %collective-permute-done.tails_ref = bf16[2,256,512]{2,1,0:T(8,128)(2,1)S(1)} collective-permute-done((bf16[2,256,512]{2,1,0:T(8,128)(2,1)}, bf16[2,256,512]{2,1,0:T(8,128)(2,1)S(1)}, u32[]{:S(2)}, u32[]{:S(2)}) %collective-permute-start) | collective-permute-done | bytes 524320 | tf_op jit(solution)/shard_map/ppermute | solution.py:326
  178.4 0.8 copy-done.12
  179.2 1.2 copy-done.5
  180.4 1.2 copy-done.7
  181.7 1.2 copy-done.9
  182.9 1.2 copy-done.11
  184.1 1.0 copy-done.13
  185.2 5.2 %shard_map.127 = (bf16[8,192,512]{2,1,0:T(8,128)(2,1)S(1)}, bf16[512,512]{1,0:T(8,128)(2,1)}) custom-call(s32[1]{0:T(128)} %bitcast.seq_ref, bf16[8,192,512]{2,1,0:T(8,128)(2,1)S(1)} %all-to-all-done.8.got_ref, bf16[512,512]{1,0:T(8,128)(2,1)S(1)} %copy-done.2, bf16[512,512]{1,0:T(8,128)(2,1)S(1)} %copy-done.3, f32[512,128]{1,0:T(8,128)S(1)} %get-tuple-element.35.f_s, ...), custom_call_target="tpu_custom_call" | custom-call | tf_op jit(solution)/shard_map/pallas_call | solution.py:270
  190.4 24.3 %all_to_all.63.got_ref = bf16[8,192,512]{2,1,0:T(8,128)(2,1)S(1)} all-to-all(bf16[8,192,512]{2,1,0:T(8,128)(2,1)S(1)} %get-tuple-element.43), channel_id=1, replica_groups=mesh['zh'=4,'zl'=2,'y'=4,'x'=4,'c'=2] {'zl','y'}, dimensions={0} | all-to-all | bytes 3145728 | tf_op jit(solution)/shard_map/all_to_all | solution.py:35
  214.7 0.2 shard_map.128
  214.9 12.1 %all_to_all.64 = bf16[4,48,512]{2,1,0:T(8,128)(2,1)S(1)} all-to-all(bf16[4,48,512]{2,1,0:T(8,128)(2,1)S(1)} %shard_map.128), channel_id=1, replica_groups=mesh['zh'=4,'zl'=2,'y'=4,'x'=4,'c'=2] {'zh'}, dimensions={0} | all-to-all | bytes 393216 | tf_op jit(solution)/shard_map/all_to_all | solution.py:35
  227.0 0.7 divide_subtract_fusion
  (36 shorter events, 0.4 us)
Async XLA Ops:
  6.2 1.0 copy-start.4
  7.2 1.0 copy-start.6
  8.1 24.9 %copy-start.8 = (f32[512,512]{1,0:T(8,128)}, f32[512,512]{1,0:T(8,128)S(1)}, u32[]{:S(2)}) copy-start(f32[512,512]{1,0:T(8,128)S(1)} %get-tuple-element.38.b_ref) | copy-start | bytes 3145732
  8.2 24.9 %copy-start.17 = (bf16[2,256,512]{2,1,0:T(8,128)(2,1)}, bf16[2,256,512]{2,1,0:T(8,128)(2,1)S(1)}, u32[]{:S(2)}) copy-start(bf16[2,256,512]{2,1,0:T(8,128)(2,1)S(1)} %get-tuple-element.40) | copy-start | bytes 1572868
  61.8 20.0 %copy-start = (bf16[512,512]{1,0:T(8,128)(2,1)S(1)}, bf16[512,512]{1,0:T(8,128)(2,1)}, u32[]{:S(2)}) copy-start(bf16[512,512]{1,0:T(8,128)(2,1)} %q_ref.5) | copy-start | bytes 1572868
  61.8 20.0 %copy-start.1 = (bf16[512,512]{1,0:T(8,128)(2,1)S(1)}, bf16[512,512]{1,0:T(8,128)(2,1)}, u32[]{:S(2)}) copy-start(bf16[512,512]{1,0:T(8,128)(2,1)} %cot_ref.3) | copy-start | bytes 1572868
  61.8 20.0 %copy-start.16 = (f32[512]{0:T(512)S(1)}, f32[512]{0:T(512)}, u32[]{:S(2)}) copy-start(f32[512]{0:T(512)} %param.13) | copy-start | bytes 6148
  96.9 1.0 copy-start.10
  134.3 11.5 %copy-start.14 = (f32[48,512]{1,0:T(8,128)}, f32[48,512]{1,0:T(8,128)S(1)}, u32[]{:S(2)}) copy-start(f32[48,512]{1,0:T(8,128)S(1)} %get-tuple-element.42) | copy-start | bytes 294916
  147.1 32.1 %copy-start.2 = (bf16[512,512]{1,0:T(8,128)(2,1)S(1)}, bf16[512,512]{1,0:T(8,128)(2,1)}, u32[]{:S(2)}) copy-start(bf16[512,512]{1,0:T(8,128)(2,1)} %k_ref.1) | copy-start | bytes 1572868
  147.1 32.1 %copy-start.3 = (bf16[512,512]{1,0:T(8,128)(2,1)S(1)}, bf16[512,512]{1,0:T(8,128)(2,1)}, u32[]{:S(2)}) copy-start(bf16[512,512]{1,0:T(8,128)(2,1)} %v_ref.1) | copy-start | bytes 1572868
  147.1 32.1 %all-to-all-start.8 = ((bf16[8,192,512]{2,1,0:T(8,128)(2,1)}), bf16[8,192,512]{2,1,0:T(8,128)(2,1)S(1)}, u32[]{:S(2)}, u32[]{:S(2)}) async-start(bf16[8,192,512]{2,1,0:T(8,128)(2,1)} %broadcast_in_dim.14), calls=%async_computation.8 | async-start | bytes 3145728 | tf_op jit(solution)/shard_map/all_to_all | solution.py:35
  153.0 25.4 %collective-permute-start = (bf16[2,256,512]{2,1,0:T(8,128)(2,1)}, bf16[2,256,512]{2,1,0:T(8,128)(2,1)S(1)}, u32[]{:S(2)}, u32[]{:S(2)}) collective-permute-start(bf16[2,256,512]{2,1,0:T(8,128)(2,1)} %copy-done.17), channel_id=1, source_target_pairs={{0,8},{8,16},{16,24},{24,32},{32,40},{40,48},{48,56},{56,64},{64,7... | collective-permute-start | bytes 1572872 | tf_op jit(solution)/shard_map/ppermute | solution.py:326
  178.4 0.8 copy-start.12
  179.2 1.2 copy-start.5
  180.4 1.2 copy-start.7
  181.7 1.2 copy-start.9
  182.9 1.2 copy-start.11
  184.1 1.0 copy-start.13
  214.7 12.3 %copy-start.15 = (f32[48,512]{1,0:T(8,128)S(1)}, f32[48,512]{1,0:T(8,128)}, u32[]{:S(2)}) copy-start(f32[48,512]{1,0:T(8,128)} %copy-done.14) | copy-start | bytes 294916
  214.7 12.3 %copy-start.18 = (f32[1,3,16,512]{3,2,1,0:T(8,128)S(1)}, f32[1,3,16,512]{3,2,1,0:T(8,128)}, u32[]{:S(2)}) copy-start(f32[1,3,16,512]{3,2,1,0:T(8,128)} %param.16) | copy-start | bytes 294916
  214.7 12.4 %copy-start.19 = (f32[1,3,16,512]{3,2,1,0:T(8,128)S(1)}, f32[1,3,16,512]{3,2,1,0:T(8,128)}, u32[]{:S(2)}) copy-start(f32[1,3,16,512]{3,2,1,0:T(8,128)} %param.17) | copy-start | bytes 294916

commit v6 on v4

--- a/solution.py
+++ b/solution.py
@@ -80,7 +80,8 @@
     parts_ref, p1_ref, p3_ref, b_ref, own_ref, tails_ref, f_s,
     w_s, d1, d3, d2, k_ref, v_ref, r_ref, w_ref, sems,
 ):
-    inputs = ((k_hbm, k_ref), (w_hbm, w_ref), (r_hbm, r_ref), (v_hbm, v_ref))
+    inputs = [(r_hbm, r_ref), (k_hbm, k_ref), (v_hbm, v_ref)]
+    inputs += [(w_hbm.at[m], w_ref.at[m]) for m in range(3)]
     fetches = [
         pltpu.make_async_copy(source, target, sems.at[number])
         for number, (source, target) in enumerate(inputs)
@@ -274,7 +275,8 @@
 
 def gather_rows(rows):
     some = swapped(rows, "zh")
-    return swapped(copies(some.reshape(-1, rows.shape[2]), NP), PLANE)
+    some = copies(some.reshape(-1, rows.shape[2]), NP)
+    return swapped(some, PLANE)
 
 
 def adam_step(weights, gradient, first_moment, second_moment):
@@ -305,7 +307,7 @@
     parts, first_pre, third_pre, back, own, tails, factors = called(
         inner_kernel, [owned, far, far, far, rows, pltpu.VMEM((2, WIN, dim), bf16), pltpu.VMEM(*side)],
         [mats, half, half, half, half, half, ((1, tokens), f32), (mats[0], f32),
-         pltpu.SemaphoreType.DMA((4,))],
+         pltpu.SemaphoreType.DMA((6,))],
         seq, *(pltpu.with_memory_space_constraint(a, pltpu.HBM) for a in (keys, values, rates, fast_init[0])),
         inputs_stay=True,
     )

time: 229 us -> 229 us (level)
  no operation moved by 1% of the time
where the time goes in v6:
time: 229 us; the launch traced here: 227 us
  blocking collectives  159 us (69%)
  waiting for transfers between devices  20.4 us (9%)
  Pallas kernels  18.4 us (8%)
  local copies, waits for them, and re-layouts  14 us (6%)
  starting transfers between devices  13.6 us (6%)
    all_to_all x9, blocking collectives, swapped(): return lax.all_to_all(parts, axes, split_axis=0, concat_axis=0, tiled=True)  159 us
    all_to_all x2, waiting for transfers between devices, swapped(): return lax.all_to_all(parts, axes, split_axis=0, concat_axis=0, tiled=True)  20.4 us
    pallas_call x9, Pallas kernels, called(): pl.pallas_call(kernel, out_shape=outs, in_specs=[place(arg, inputs_stay)...  18.4 us
    unnamed x50, local copies, waits for them, and re-layouts  12.6 us
    all_to_all x2, starting transfers between devices, swapped(): return lax.all_to_all(parts, axes, split_axis=0, concat_axis=0, tiled=True)  10.1 us
  transfers between devices with their start and end apart: 3, of which 2 were waited for; matrix products, arithmetic and copies ran while one was open for 0% of the time, Pallas kernels for 1%

profile of v6, /device:TPU:24, one launch (start us, length us, event | category | flops | bytes accessed | tf_op | source)
XLA Modules:
  0.0 227.0 jit_solution(2808880263745746963)
XLA Ops:
  0.6 5.3 %shard_map.120 = (bf16[8,192,512]{2,1,0:T(8,128)(2,1)S(1)}, f32[512,512]{1,0:T(8,128)S(1)}, f32[512,512]{1,0:T(8,128)S(1)}, f32[512,512]{1,0:T(8,128)S(1)}, f32[...) custom-call(s32[1]{0:T(128)} %bitcast.seq_ref, bf16[512,512]{1,0:T(8,128)(2,1)} %k_ref.3, ...), custom_call_target="tpu_custom_call" | custom-call | tf_op jit(solution)/shard_map/pallas_call | solution.py:259
  6.0 1.0 copy-done.11
  6.9 1.0 copy-done.13
  7.9 24.9 %all_to_all.55.got_ref = bf16[8,192,512]{2,1,0:T(8,128)(2,1)S(1)} all-to-all(bf16[8,192,512]{2,1,0:T(8,128)(2,1)S(1)} %get-tuple-element.22), channel_id=1, replica_groups=mesh['zh'=4,'zl'=2,'y'=4,'x'=4,'c'=2] {'zl','y'}, dimensions={0} | all-to-all | bytes 3145728 | tf_op jit(solution)/shard_map/all_to_all | solution.py:35
  33.0 16.8 %all_to_all.56.got_ref = bf16[4,48,512]{2,1,0:T(8,128)(2,1)S(1)} all-to-all(bf16[4,48,512]{2,1,0:T(8,128)(2,1)S(1)} %shard_map.121), channel_id=1, replica_groups=mesh['zh'=4,'zl'=2,'y'=4,'x'=4,'c'=2] {'zh'}, dimensions={0} | all-to-all | bytes 393216 | tf_op jit(solution)/shard_map/all_to_all | solution.py:35
  50.0 11.4 %all_to_all.57 = bf16[4,48,512]{2,1,0:T(8,128)(2,1)S(1)} all-to-all(bf16[4,48,512]{2,1,0:T(8,128)(2,1)S(1)} %get-tuple-element.24), channel_id=1, replica_groups=mesh['zh'=4,'zl'=2,'y'=4,'x'=4,'c'=2] {'zh'}, dimensions={0} | all-to-all | bytes 393216 | tf_op jit(solution)/shard_map/all_to_all | solution.py:35
  61.4 1.3 broadcast_in_dim.12
  62.7 5.8 %all-to-all-start.3 = ((bf16[8,192,512]{2,1,0:T(8,128)(2,1)}), bf16[8,192,512]{2,1,0:T(8,128)(2,1)S(1)}, u32[]{:S(2)}, u32[]{:S(2)}) async-start(bf16[8,192,512]{2,1,0:T(8,128)(2,1)} %broadcast_in_dim.12), calls=%async_computation.3 | async-start | bytes 3145728 | tf_op jit(solution)/shard_map/all_to_all | solution.py:35
  68.5 3.5 %collective-permute-start = (bf16[2,256,512]{2,1,0:T(8,128)(2,1)}, bf16[2,256,512]{2,1,0:T(8,128)(2,1)}, u32[]{:S(2)}, u32[]{:S(2)}) collective-permute-start(bf16[2,256,512]{2,1,0:T(8,128)(2,1)} %copy-done.22), channel_id=1, source_target_pairs={{0,8},{8,16},{16,24},{24,32},{32,40},{40,48},{48,56},{56,64},{64,7... | collective-permute-start | bytes 1572872 | tf_op jit(solution)/shard_map/ppermute | solution.py:315
  72.0 14.9 %all-to-all-done.3.got_ref = bf16[8,192,512]{2,1,0:T(8,128)(2,1)S(1)} async-done(((bf16[8,192,512]{2,1,0:T(8,128)(2,1)}), bf16[8,192,512]{2,1,0:T(8,128)(2,1)S(1)}, u32[]{:S(2)}, u32[]{:S(2)}) %all-to-all-start.3) | async-done | bytes 1572896 | tf_op jit(solution)/shard_map/all_to_all | solution.py:35
  86.9 1.0 copy-done.3
  88.0 3.3 %shard_map.123 = (f32[512,512]{1,0:T(8,128)S(1)}, f32[512,512]{1,0:T(8,128)S(1)}, f32[512,512]{1,0:T(8,128)S(1)}, f32[8,2,512]{2,1,0:T(2,128)}, bf16[512,512]{1,0:T(8,128)(2,1)S(1)}) custom-call(bf16[8,192,512]{2,1,0:T(8,128)(2,1)S(1)} %all-to-all-done.3.got_ref, bf16[512,512]{1,0:T(8,128)(2,1)S(1)} %copy-done.2, bf16[512,512]{1,0:T(8,128)(2,1)S(1)} %copy-done.3, ...), custom_call_target="tpu_custom_call" | custom-call | tf_op jit(solution)/shard_map/pallas_call | solution.py:259
  91.3 1.0 copy-done.5
  92.4 1.0 copy-done.7
  93.4 1.0 copy-done.9
  94.3 0.8 copy-done.17
  95.1 4.3 %all-to-all-start.4 = ((f32[8,2,512]{2,1,0:T(2,128)}), f32[8,2,512]{2,1,0:T(2,128)S(1)}, u32[]{:S(2)}, u32[]{:S(2)}) async-start(f32[8,2,512]{2,1,0:T(2,128)} %get-tuple-element.25), calls=%async_computation.4 | async-start | bytes 65536 | tf_op jit(solution)/shard_map/all_to_all | solution.py:35
  99.4 5.4 %all-to-all-done.4.sums_ref = f32[8,2,512]{2,1,0:T(2,128)S(1)} async-done(((f32[8,2,512]{2,1,0:T(2,128)}), f32[8,2,512]{2,1,0:T(2,128)S(1)}, u32[]{:S(2)}, u32[]{:S(2)}) %all-to-all-start.4) | async-done | bytes 32800 | tf_op jit(solution)/shard_map/all_to_all | solution.py:35
  104.9 1.0 copy-done.4
  105.9 1.2 copy-done.6
  107.1 1.2 copy-done.8
  108.4 1.2 copy-done.10
  109.6 1.0 copy-done.18
  110.6 5.5 %shard_map.124 = (bf16[8,192,512]{2,1,0:T(8,128)(2,1)S(1)}, bf16[512,512]{1,0:T(8,128)(2,1)}) custom-call(s32[1]{0:T(128)} %bitcast.seq_ref, f32[8,2,512]{2,1,0:T(2,128)S(1)} %all-to-all-done.4.sums_ref, f32[512,512]{1,0:T(8,128)S(1)} %copy-done.6, f32[512,512]{1,0:T(8,128)S(1)} %copy-done.8, f32[512,512]{1,0:T(8,128)S(1)} %copy-done.10, ...), custom_call_target="tpu_custom_call" | custom-call | tf_op jit(solution)/shard_map/pallas_call | solution.py:259
  116.2 25.1 %all_to_all.58.got_ref = bf16[8,192,512]{2,1,0:T(8,128)(2,1)S(1)} all-to-all(bf16[8,192,512]{2,1,0:T(8,128)(2,1)S(1)} %get-tuple-element.32), channel_id=1, replica_groups=mesh['zh'=4,'zl'=2,'y'=4,'x'=4,'c'=2] {'zl','y'}, dimensions={0} | all-to-all | bytes 3145728 | tf_op jit(solution)/shard_map/all_to_all | solution.py:35
  141.5 17.3 %all_to_all.59.got_ref = bf16[4,48,512]{2,1,0:T(8,128)(2,1)S(1)} all-to-all(bf16[4,48,512]{2,1,0:T(8,128)(2,1)S(1)} %shard_map.125), channel_id=1, replica_groups=mesh['zh'=4,'zl'=2,'y'=4,'x'=4,'c'=2] {'zh'}, dimensions={0} | all-to-all | bytes 393216 | tf_op jit(solution)/shard_map/all_to_all | solution.py:35
  159.0 11.5 %all_to_all.60 = bf16[4,48,512]{2,1,0:T(8,128)(2,1)S(1)} all-to-all(bf16[4,48,512]{2,1,0:T(8,128)(2,1)S(1)} %get-tuple-element.35), channel_id=1, replica_groups=mesh['zh'=4,'zl'=2,'y'=4,'x'=4,'c'=2] {'zh'}, dimensions={0} | all-to-all | bytes 393216 | tf_op jit(solution)/shard_map/all_to_all | solution.py:35
  170.7 20.2 %all_to_all.61.got_ref = bf16[8,192,512]{2,1,0:T(8,128)(2,1)S(1)} all-to-all(bf16[8,192,512]{2,1,0:T(8,128)(2,1)S(1)} %broadcast_in_dim.14), channel_id=1, replica_groups=mesh['zh'=4,'zl'=2,'y'=4,'x'=4,'c'=2] {'zl','y'}, dimensions={0} | all-to-all | bytes 3145728 | tf_op jit(solution)/shard_map/all_to_all | solution.py:35
  190.8 3.3 %shard_map.127 = bf16[8,192,512]{2,1,0:T(8,128)(2,1)S(1)} custom-call(bf16[8,192,512]{2,1,0:T(8,128)(2,1)S(1)} %all_to_all.61.got_ref, bf16[512,512]{1,0:T(8,128)(2,1)S(1)} %copy-done, bf16[512,512]{1,0:T(8,128)(2,1)S(1)} %copy-done.1, f32[512,128]{1,0:T(8,128)S(1)} %get-tuple-element.36.f_s, f32[512,512]{1,0:T(8,128)S(1)} %copy-done.12, ...), custom_call_target="tpu_custom_call" | custom-call | tf_op jit(solution)/shard_map/pallas_call | solution.py:259
  194.1 18.3 %all_to_all.62.got_ref = bf16[8,192,512]{2,1,0:T(8,128)(2,1)S(1)} all-to-all(bf16[8,192,512]{2,1,0:T(8,128)(2,1)S(1)} %shard_map.127), channel_id=1, replica_groups=mesh['zh'=4,'zl'=2,'y'=4,'x'=4,'c'=2] {'zl','y'}, dimensions={0} | all-to-all | bytes 3145728 | tf_op jit(solution)/shard_map/all_to_all | solution.py:35
  212.7 13.5 %all_to_all.63 = bf16[4,48,512]{2,1,0:T(8,128)(2,1)S(1)} all-to-all(bf16[4,48,512]{2,1,0:T(8,128)(2,1)S(1)} %shard_map.128), channel_id=1, replica_groups=mesh['zh'=4,'zl'=2,'y'=4,'x'=4,'c'=2] {'zh'}, dimensions={0} | all-to-all | bytes 393216 | tf_op jit(solution)/shard_map/all_to_all | solution.py:35
  226.3 0.7 divide_subtract_fusion
  (47 shorter events, 1.1 us)
Async XLA Ops:
  6.0 1.0 copy-start.11
  6.9 1.0 copy-start.13
  7.9 24.9 %copy-start.15 = (f32[512,512]{1,0:T(8,128)}, f32[512,512]{1,0:T(8,128)S(1)}, u32[]{:S(2)}) copy-start(f32[512,512]{1,0:T(8,128)S(1)} %get-tuple-element.39.b_ref) | copy-start | bytes 3145732
  7.9 24.9 %copy-start.22 = (bf16[2,256,512]{2,1,0:T(8,128)(2,1)}, bf16[2,256,512]{2,1,0:T(8,128)(2,1)S(1)}, u32[]{:S(2)}) copy-start(bf16[2,256,512]{2,1,0:T(8,128)(2,1)S(1)} %get-tuple-element.30) | copy-start | bytes 1572868
  50.0 11.5 %copy-start.19 = (f32[48,512]{1,0:T(8,128)}, f32[48,512]{1,0:T(8,128)S(1)}, u32[]{:S(2)}) copy-start(f32[48,512]{1,0:T(8,128)S(1)} %get-tuple-element.33.moved_ref) | copy-start | bytes 294916
  62.7 24.2 %copy-start.2 = (bf16[512,512]{1,0:T(8,128)(2,1)S(1)}, bf16[512,512]{1,0:T(8,128)(2,1)}, u32[]{:S(2)}) copy-start(bf16[512,512]{1,0:T(8,128)(2,1)} %q_ref.3) | copy-start | bytes 1572868
  62.7 24.2 %copy-start.21 = (f32[512]{0:T(512)S(1)}, f32[512]{0:T(512)}, u32[]{:S(2)}) copy-start(f32[512]{0:T(512)} %param.13) | copy-start | bytes 6148
  62.7 24.2 %all-to-all-start.3 = ((bf16[8,192,512]{2,1,0:T(8,128)(2,1)}), bf16[8,192,512]{2,1,0:T(8,128)(2,1)S(1)}, u32[]{:S(2)}, u32[]{:S(2)}) async-start(bf16[8,192,512]{2,1,0:T(8,128)(2,1)} %broadcast_in_dim.12), calls=%async_computation.3 | async-start | bytes 3145728 | tf_op jit(solution)/shard_map/all_to_all | solution.py:35
  68.5 36.4 %copy-start = (bf16[512,512]{1,0:T(8,128)(2,1)S(1)}, bf16[512,512]{1,0:T(8,128)(2,1)}, u32[]{:S(2)}) copy-start(bf16[512,512]{1,0:T(8,128)(2,1)} %k_ref.3) | copy-start | bytes 1572868
  68.5 36.4 %copy-start.1 = (bf16[512,512]{1,0:T(8,128)(2,1)S(1)}, bf16[512,512]{1,0:T(8,128)(2,1)}, u32[]{:S(2)}) copy-start(bf16[512,512]{1,0:T(8,128)(2,1)} %v_ref.3) | copy-start | bytes 1572868
  68.5 30.9 %collective-permute-start = (bf16[2,256,512]{2,1,0:T(8,128)(2,1)}, bf16[2,256,512]{2,1,0:T(8,128)(2,1)}, u32[]{:S(2)}, u32[]{:S(2)}) collective-permute-start(bf16[2,256,512]{2,1,0:T(8,128)(2,1)} %copy-done.22), channel_id=1, source_target_pairs={{0,8},{8,16},{16,24},{24,32},{32,40},{40,48},{48,56},{56,64},{64,7... | collective-permute-start | bytes 1572872 | tf_op jit(solution)/shard_map/ppermute | solution.py:315
  86.9 1.0 copy-start.3
  91.3 1.0 copy-start.5
  92.4 1.0 copy-start.7
  93.4 1.0 copy-start.9
  94.3 0.8 copy-start.17
  95.1 9.8 %all-to-all-start.4 = ((f32[8,2,512]{2,1,0:T(2,128)}), f32[8,2,512]{2,1,0:T(2,128)S(1)}, u32[]{:S(2)}, u32[]{:S(2)}) async-start(f32[8,2,512]{2,1,0:T(2,128)} %get-tuple-element.25), calls=%async_computation.4 | async-start | bytes 65536 | tf_op jit(solution)/shard_map/all_to_all | solution.py:35
  104.9 1.0 copy-start.4
  105.9 1.2 copy-start.6
  107.1 1.2 copy-start.8
  108.4 1.2 copy-start.10
  109.6 1.0 copy-start.18
  141.3 17.6 %copy-start.20 = (f32[48,512]{1,0:T(8,128)S(1)}, f32[48,512]{1,0:T(8,128)}, u32[]{:S(2)}) copy-start(f32[48,512]{1,0:T(8,128)} %copy-done.19) | copy-start | bytes 294916
  170.6 20.2 %copy-start.12 = (f32[512,512]{1,0:T(8,128)S(1)}, f32[512,512]{1,0:T(8,128)}, u32[]{:S(2)}) copy-start(f32[512,512]{1,0:T(8,128)} %copy-done.11) | copy-start | bytes 3145732
  170.6 20.2 %copy-start.14 = (f32[512,512]{1,0:T(8,128)S(1)}, f32[512,512]{1,0:T(8,128)}, u32[]{:S(2)}) copy-start(f32[512,512]{1,0:T(8,128)} %copy-done.13) | copy-start | bytes 3145732
  170.6 20.2 %copy-start.16 = (f32[512,512]{1,0:T(8,128)S(1)}, f32[512,512]{1,0:T(8,128)}, u32[]{:S(2)}) copy-start(f32[512,512]{1,0:T(8,128)} %copy-done.15) | copy-start | bytes 3145732
  212.5 13.8 %copy-start.23 = (f32[1,3,16,512]{3,2,1,0:T(8,128)S(1)}, f32[1,3,16,512]{3,2,1,0:T(8,128)}, u32[]{:S(2)}) copy-start(f32[1,3,16,512]{3,2,1,0:T(8,128)} %param.16) | copy-start | bytes 294916
  212.5 13.8 %copy-start.24 = (f32[1,3,16,512]{3,2,1,0:T(8,128)S(1)}, f32[1,3,16,512]{3,2,1,0:T(8,128)}, u32[]{:S(2)}) copy-start(f32[1,3,16,512]{3,2,1,0:T(8,128)} %param.17) | copy-start | bytes 294916
